TPU v7x, 32 devices: a whole 2x2x4 slice. The times are simulated.
32 devices in a mesh: dp: 8 (over y, x, core), tensor: 4 (over z).
Axes of the slice: x: 2, y: 2, z: 4, core: 2. Of those that a mesh axis runs over, the one named last changes fastest.
Arguments:
- tokens: bfloat16 [16384, 768], P(('dp', 'tensor')), may hold values from -6 to 6
- cotangent: bfloat16 [16384, 768], P(('dp', 'tensor')), may hold values from -6 to 6
- lengths: int32 [8], P('dp'), may hold values from 1025 to 2048, as said below
- query_weight: bfloat16 [768, 768], P('dp', 'tensor'), may hold values from -0.3125 to 0.3125
- key_weight: bfloat16 [768, 768], P('dp', 'tensor'), may hold values from -0.3125 to 0.3125
- value_weight: bfloat16 [768, 768], P('dp', 'tensor'), may hold values from -0.21875 to 0.21875
- query_bias: bfloat16 [64, 12], P('dp', 'tensor'), may hold values from -1.796875 to 1.796875
- value_bias: bfloat16 [64, 12], P('dp', 'tensor'), may hold values from -0.59765625 to 0.59765625
- output_weight: bfloat16 [768, 768], P('dp', 'tensor'), may hold values from -0.875 to 0.875
- output_bias: bfloat16 [768], P('dp'), may hold values from -1.796875 to 1.796875
- first_gain: bfloat16 [768], P('dp'), may hold values from 0.5 to 1.5
- first_shift: bfloat16 [768], P('dp'), may hold values from -1.796875 to 1.796875
- inner_weight: bfloat16 [768, 3072], P('dp', 'tensor'), may hold values from -0.21875 to 0.21875
- inner_bias: bfloat16 [64, 48], P('dp', 'tensor'), may hold values from -1.796875 to 1.796875
- outer_weight: bfloat16 [768, 3072], P('dp', 'tensor'), may hold values from -0.109375 to 0.109375
- outer_bias: bfloat16 [768], P('dp'), may hold values from -1.796875 to 1.796875
- second_gain: bfloat16 [768], P('dp'), may hold values from 0.5 to 1.5
- second_shift: bfloat16 [768], P('dp'), may hold values from -1.796875 to 1.796875
Outputs:
- layer_out: bfloat16 [16384, 768], P(('dp', 'tensor'))
- tokens_gradient: float32 [16384, 768], P(('dp', 'tensor'))
- query_weight_gradient: float32 [768, 768], P('dp', 'tensor')
- key_weight_gradient: float32 [768, 768], P('dp', 'tensor')
- value_weight_gradient: float32 [768, 768], P('dp', 'tensor')
- query_bias_gradient: float32 [64, 12], P('dp', 'tensor')
- value_bias_gradient: float32 [64, 12], P('dp', 'tensor')
- output_weight_gradient: float32 [768, 768], P('dp', 'tensor')
- output_bias_gradient: float32 [768], P('dp')
- first_gain_gradient: float32 [768], P('dp')
- first_shift_gradient: float32 [768], P('dp')
- inner_weight_gradient: float32 [768, 3072], P('dp', 'tensor')
- inner_bias_gradient: float32 [64, 48], P('dp', 'tensor')
- outer_weight_gradient: float32 [768, 3072], P('dp', 'tensor')
- outer_bias_gradient: float32 [768], P('dp')
- second_gain_gradient: float32 [768], P('dp')
- second_shift_gradient: float32 [768], P('dp')
Inputs may be any that keep to these rules, and one draw needn't show every extreme that they name: lengths[s] is the number of valid tokens at the start of slot s; some slot is full and some holds exactly 1025.
All inputs are finite; a program needn't handle non-finite values.
Results may differ from a plain program's by a relative error of at most 0.014.
The roundings to bfloat16 on the way count: a program that leaves them out, or rounds other values in their place, can miss the bound.
Values may be sent and summed in bfloat16 or wider, within the bound.
No kernel may reach another device: no remote copies, remote signals or barrier semaphores. Data moves between devices by JAX's collectives and lax.ppermute only.
A program may use at most 128 MiB of HBM per device.

v0:
```python
import functools
import math

import jax
import jax.numpy as jnp
from jax import lax
from jax.experimental import pallas as pl
from jax.experimental.pallas import tpu as pltpu
from jax.sharding import PartitionSpec as P

HD = 64
SLOT_LEN = 2048
EPS = 1e-05
NEG = -1e30
BF = jnp.bfloat16
F32 = jnp.float32
VMEM_LIMIT = 60 * 1024 * 1024
LIGHT = pl.CostEstimate(flops=1, transcendentals=0, bytes_accessed=1)


def dot(a, b, ca, cb):
    return lax.dot_general(a, b, (((ca,), (cb,)), ((), ())), preferred_element_type=F32)


def whole(shape):
    return pl.BlockSpec(shape, lambda *_: (0,) * len(shape))


def params():
    return pltpu.CompilerParams(vmem_limit_bytes=VMEM_LIMIT)


def swap(x, axis, mask):
    n = lax.axis_size(axis)
    return lax.ppermute(x, axis, [(i, i ^ mask) for i in range(n)])


def dp_groups():
    n, bit, groups = lax.axis_size("dp"), 2, []
    while bit < n:
        if bit * 2 < n:
            groups.append((bit, bit * 2, bit * 3))
            bit *= 4
        else:
            groups.append((bit,))
            bit *= 2
    return groups


def stage(*values):
    return lax.optimization_barrier(values)


def shift(x, by):
    n = lax.axis_size("tensor")
    return lax.ppermute(x, "tensor", [(i, i + by) for i in range(n) if 0 <= i + by < n])


def by_slot(up, down, k):
    z = lax.axis_index("tensor")
    odd, high = z % 2 == 1, z >= 2
    if k == 0:
        return up[0]
    if k == 1:
        return jnp.where(odd, up[1], down[1])
    if k == 2:
        return jnp.where(high, up[2], down[2])
    return jnp.where(odd, jnp.where(high, up[3], down[1]), jnp.where(high, up[1], down[3]))


def exchange(blocks):
    return lax.all_to_all(blocks, "tensor", 0, 0)


def aligned(rows):
    return rows % 16 == 0 and lax.axis_size("dp") == 8


def gather_all(piece):
    n, t = lax.axis_size("dp"), lax.axis_size("tensor")
    rows, cols = piece.shape
    blocks = lax.all_gather(piece, ("dp", "tensor")).reshape(n, t, rows, cols)
    if aligned(rows):
        return blocks
    return blocks.transpose(1, 0, 2, 3).reshape(1, t, n * rows, cols)


def gather_rows(piece):
    rows, cols = piece.shape
    n = lax.axis_size("dp")
    me = lax.axis_index("dp")
    pieces = [((0,), piece)]
    for group in dp_groups():
        if len(pieces) > 1:
            pieces = [(sum((m for m, _ in pieces), ()), jnp.concatenate([a for _, a in pieces], axis=0))]
        masks, array = pieces[0]
        pieces += [(tuple(m ^ g for m in masks), swap(array, "dp", g)) for g in group]
    pieces += [(tuple(m ^ 1 for m in masks), swap(array, "dp", 1)) for masks, array in pieces]
    order = [m for masks, _ in pieces for m in masks]
    place = [order.index(m) for m in range(n)]
    stacked = jnp.concatenate([a for _, a in pieces], axis=0).reshape(n, rows, cols)
    index = jnp.take(jnp.array(place, jnp.int32), me ^ jnp.arange(n))
    return jnp.take(stacked, index, axis=0).reshape(n * rows, cols)


def put(where, refs, out):
    if len(refs) == 1:
        out[...] = refs[0][...]
        return
    count = out.shape[0] // refs[0].shape[0]
    each = (where.shape[0] if hasattr(where, "shape") else len(where)) // count
    rows = refs[0].shape[0] // each
    for s, ref in enumerate(refs):
        for b in range(each):
            out[pl.ds(pl.multiple_of(where[each * s + b], rows), rows), :] = ref[b * rows : (b + 1) * rows]


def assemble_kernel(where, *refs):
    put(where, refs[:-1], refs[-1])


def assemble(pieces, where, block, at):
    rows, n = pieces[0].shape[0], len(pieces)
    return pl.pallas_call(
        assemble_kernel,
        out_shape=jax.ShapeDtypeStruct((n * rows, block), pieces[0].dtype),
        grid_spec=pltpu.PrefetchScalarGridSpec(
            num_scalar_prefetch=1,
            grid=(1,),
            in_specs=[pl.BlockSpec((rows, block), lambda i, w: (0, at))] * n,
            out_specs=pl.BlockSpec((n * rows, block), lambda i, w: (0, 0)),
        ),
        compiler_params=params(),
        cost_estimate=LIGHT,
        name="assemble",
    )(where, *pieces)


def split_rows(place, value, keep, send, lane):
    lanes = slice(lane, lane + value.shape[1])
    if send is None:
        keep[:, lanes] = value
        return
    rows = keep.shape[1]
    for j in range(4):
        at = jnp.bitwise_xor(j, place[1])
        even, odd = value[2 * j * rows : (2 * j + 1) * rows], value[(2 * j + 1) * rows : (2 * j + 2) * rows]
        keep[at, :, lanes] = jnp.where(place[0] == 0, even, odd)
        send[at, :, lanes] = jnp.where(place[0] == 0, odd, even)


def add_kernel(groups, *refs):
    outs = refs[len(refs) - len(groups) :]
    for out, terms in zip(outs, groups, strict=True):
        total = refs[terms[0]][...].astype(F32)
        for t in terms[1:]:
            total = total + refs[t][...].astype(F32)
        out[...] = total.reshape(out.shape).astype(out.dtype)


def add(terms, outs):
    lanes = outs[0][1]
    block = 1792
    specs = []
    for array, lead, start in terms:
        rows = array.shape[-2]
        if lead is None:
            specs.append(pl.BlockSpec((rows, block), lambda i, s=start // block: (0, i + s)))
        else:
            specs.append(pl.BlockSpec((1, rows, block), lambda i, m=lead, s=start // block: (m, 0, i + s)))
    rows = terms[0][0].shape[-2]
    return pl.pallas_call(
        functools.partial(add_kernel, [numbers for numbers, _, _ in outs]),
        grid=(lanes // block,),
        out_shape=[jax.ShapeDtypeStruct((rows, lanes), d) for _, _, d in outs],
        in_specs=specs,
        out_specs=[pl.BlockSpec((rows, block), lambda i: (0, i))] * len(outs),
        compiler_params=params(),
        cost_estimate=LIGHT,
        name="add",
    )(*[a for a, _, _ in terms])


def sum_rows(array):
    n = lax.axis_size("dp")
    me = lax.axis_index("dp")
    halves = array.reshape(n // 2, 2, array.shape[0] // n, array.shape[1])
    side = lambda c: lax.dynamic_index_in_dim(halves, c, 1, keepdims=False)
    total = side(me & 1).astype(F32) + swap(side(1 - (me & 1)), "dp", 1).astype(F32)
    for group in reversed(dp_groups()):
        count = len(group) + 1
        total = total.reshape(count, -1, *total.shape[1:])
        mine = (me // group[0]) % count
        sent = total.astype(BF)
        terms = [swap(pick(sent, mine ^ (g // group[0])), "dp", g).astype(F32) for g in group]
        total = pick(total, mine)
        for t in terms:
            total = total + t
    return total.reshape(total.shape[-2:])


def pick(array, index):
    return lax.dynamic_index_in_dim(array, index, 0, keepdims=False)


def split_shapes(aligned_rows, rows, cols):
    shape = jax.ShapeDtypeStruct
    return [shape((4, rows, cols), BF)] * 2 if aligned_rows else [shape((768, cols), BF)]


def spread(rows, few):
    i = lax.broadcasted_iota(jnp.int32, (768, HD), 1)
    r = lax.broadcasted_iota(jnp.int32, (768, HD), 0)
    return (r == (i // few) * rows + i % few).astype(F32).astype(BF)


def project_kernel(where, x_ref, b_ref, *refs):
    pieces, (qt_ref, q_ref, kv_ref, kvt_ref, w) = refs[:-5], refs[-5:]
    put(where, pieces, w)
    y = dot(x_ref[...], w[...], 1, 0) + b_ref[0]
    keep = lax.broadcasted_iota(jnp.int32, (512, 128), 1) < HD
    q = jnp.where(keep, y[:, :128].astype(BF).astype(F32) * 0.125, 0.0).astype(BF)
    kv = y[:, 128:].astype(BF)
    q_ref[0] = q
    qt_ref[0] = q.T
    kv_ref[0] = kv
    kvt_ref[0] = kv.T


def project(x, near, bias):
    pieces, where = near
    heads, rows = bias.shape[0], pieces[0].shape[0]
    shapes = [(heads, 128, 512), (heads, 512, 128), (heads, 512, 128), (heads, 128, 512)]
    return pl.pallas_call(
        project_kernel,
        out_shape=[jax.ShapeDtypeStruct(s, BF) for s in shapes],
        grid_spec=pltpu.PrefetchScalarGridSpec(
            num_scalar_prefetch=1,
            grid=(heads,),
            in_specs=[whole((512, 768)), pl.BlockSpec((1, 1, 256), lambda h, w: (h, 0, 0))]
            + [pl.BlockSpec((rows, 256), lambda h, w: (0, h))] * len(pieces),
            out_specs=[pl.BlockSpec((1, *s[1:]), lambda h, w: (h, 0, 0)) for s in shapes],
            scratch_shapes=[pltpu.VMEM((768, 256), BF)],
        ),
        compiler_params=params(),
        cost_estimate=LIGHT,
        name="project",
    )(where, x, bias, *pieces)


def masked(scores, count):
    return jnp.where(lax.broadcasted_iota(jnp.int32, scores.shape, 0) < count, scores, NEG)


def attend_kernel(counts, qt_ref, k0, k1, k2, k3, t0, t1, t2, t3, mt_ref, lse_ref):
    h = pl.program_id(0)
    qt = qt_ref[0]
    kvt = (t0, t1, t2, t3)
    scores = [masked(dot(k[0], qt, 1, 0), counts[j]) for j, k in enumerate((k0, k1, k2, k3))]
    peak = functools.reduce(jnp.maximum, [jnp.max(s, axis=0, keepdims=True) for s in scores])
    total = jnp.zeros((1, 512), F32)
    acc = jnp.zeros((128, 512), F32)
    for j in range(4):
        expo = jnp.exp(scores[j] - peak)
        total = total + jnp.sum(expo, axis=0, keepdims=True)
        acc = acc + dot(kvt[j][0], expo.astype(BF), 1, 0)
    mt_ref[pl.ds(pl.multiple_of(h * HD, HD), HD), :] = (acc[HD:] / total).astype(BF)
    lse_ref[0] = peak + jnp.log(total)


def attend(counts, qt, kv, kvt):
    heads = qt.shape[0]
    return pl.pallas_call(
        attend_kernel,
        out_shape=[jax.ShapeDtypeStruct((heads * HD, 512), BF), jax.ShapeDtypeStruct((heads, 1, 512), F32)],
        grid_spec=pltpu.PrefetchScalarGridSpec(
            num_scalar_prefetch=1,
            grid=(heads,),
            in_specs=[pl.BlockSpec((1, 128, 512), lambda h, c: (h, 0, 0))]
            + [pl.BlockSpec((1, 512, 128), lambda h, c: (h, 0, 0))] * 4
            + [pl.BlockSpec((1, 128, 512), lambda h, c: (h, 0, 0))] * 4,
            out_specs=[
                pl.BlockSpec((heads * HD, 512), lambda h, c: (0, 0)),
                pl.BlockSpec((1, 1, 512), lambda h, c: (h, 0, 0)),
            ],
        ),
        compiler_params=params(),
        cost_estimate=LIGHT,
        name="attend",
    )(counts, qt, *kv, *kvt)


def back_step(counts, qt, q, kv, kvt, dot_rows, lse, dkv_ref, fresh):
    dt = jnp.concatenate([jnp.zeros((HD, 512), BF), dot_rows], axis=0)
    d = dt.T
    probs, grads = [], []
    inner = jnp.zeros((1, 512), F32)
    for j in range(4):
        p = jnp.exp(masked(dot(kv[j][0], qt, 1, 0), counts[j]) - lse)
        g = dot(kv[j][0], dt, 1, 0)
        inner = inner + jnp.sum(p * g, axis=0, keepdims=True)
        probs.append(p)
        grads.append(g)
    dqt = jnp.zeros((128, 512), F32)
    for j in range(4):
        ds = (probs[j] * (grads[j] - inner)).astype(BF)
        dqt = dqt + dot(kvt[j][0], ds, 1, 0)
        dkv = dot(ds, q, 1, 0) + dot(probs[j].astype(BF), d, 1, 0)
        if fresh is None:
            dkv_ref[j] = dkv
        else:
            dkv_ref[j] = dkv_ref[j] + dkv
    return dqt[:HD] * 0.125


def back_own_kernel(counts, qt_ref, q_ref, *refs):
    kv, kvt, (dt_ref, lse_ref, dqt_ref, dkv_ref, bias_ref) = refs[:4], refs[4:8], refs[8:]
    dqt = back_step(counts, qt_ref[0], q_ref[0], kv, kvt, dt_ref[0], lse_ref[0], dkv_ref.at[0], None)
    dqt_ref[0] = dqt.astype(BF)
    bias_ref[0] = jnp.sum(dqt, axis=1, keepdims=True)


def back_own(counts, qt, q, kv, kvt, dt, lse):
    heads = qt.shape[0]
    tall, flat = pl.BlockSpec((1, 512, 128), lambda h, c: (h, 0, 0)), pl.BlockSpec((1, 128, 512), lambda h, c: (h, 0, 0))
    return pl.pallas_call(
        back_own_kernel,
        out_shape=[
            jax.ShapeDtypeStruct((heads, HD, 512), BF),
            jax.ShapeDtypeStruct((heads, 4, 512, 128), F32),
            jax.ShapeDtypeStruct((heads, HD, 1), F32),
        ],
        grid_spec=pltpu.PrefetchScalarGridSpec(
            num_scalar_prefetch=1,
            grid=(heads,),
            in_specs=[flat, tall]
            + [tall] * 4
            + [flat] * 4
            + [
                pl.BlockSpec((1, HD, 512), lambda h, c: (c[6], h, 0)),
                pl.BlockSpec((1, 1, 512), lambda h, c: (h, 0, 0)),
            ],
            out_specs=[
                pl.BlockSpec((1, HD, 512), lambda h, c: (h, 0, 0)),
                pl.BlockSpec((1, 4, 512, 128), lambda h, c: (h, 0, 0, 0)),
                pl.BlockSpec((1, HD, 1), lambda h, c: (h, 0, 0)),
            ],
        ),
        compiler_params=params(),
        cost_estimate=LIGHT,
        name="back_own",
    )(counts, qt, q, *kv, *kvt, dt, lse)


def back_head_kernel(few, apart, sc, *refs):
    qts, qs, kv, kvt = refs[:3], refs[3:6], refs[6:10], refs[10:14]
    ds, ls, (dq0_ref, dkv_ref, b_ref), xs = refs[14:17], refs[17:20], refs[20:23], refs[23:27]
    packet, outs, (acc, dqs, qb) = refs[27], refs[28:-3], refs[-3:]
    s = pl.program_id(0)

    @pl.when(s == 0)
    def _():
        acc[...] = dkv_ref[0]
        dqs[0] = dq0_ref[0]
        qb[...] = b_ref[0]

    choose = lambda a: jnp.where(s == 0, a[0], jnp.where(s == 1, a[1], a[2]))
    rows = choose([d[0] for d in ds])
    lse = choose([v[0] for v in ls])
    qt, q = choose([v[0] for v in qts]), choose([v[0] for v in qs])
    dqt = back_step(sc, qt, q, kv, kvt, rows, lse, acc, True)
    dqs[s + 1] = dqt.astype(BF)
    qb[...] += jnp.sum(dqt, axis=1, keepdims=True)

    @pl.when(s == 2)
    def _():
        dwt = jnp.zeros((256, 768), F32)
        vsum = jnp.zeros((1, 128), F32)
        for j in range(4):
            part = acc[j]
            vsum = vsum + jnp.sum(part, axis=0, keepdims=True)
            both = jnp.concatenate([dqs[j], part.astype(BF).T], axis=0)
            packet[jnp.bitwise_xor(sc[6], j)] = both
            both = jnp.concatenate([both, jnp.zeros((HD, 512), BF)], axis=0)
            dwt = dwt + dot(both, xs[j][...], 1, 0)
        lane = lax.broadcasted_iota(jnp.int32, (HD, 256), 1)
        vcol = jnp.broadcast_to(vsum, (128, 128)).T[HD:, :1]
        sums = jnp.where(lane == 192, qb[...], jnp.where(lane == 193, vcol, 0.0)).astype(BF)
        rows = 768 * few // HD
        dw = dwt.T + dot(spread(rows, few), sums, 1, 0)
        split_rows((sc[4], sc[5]), dw.astype(BF), outs[0], outs[1] if apart else None, 0)


def back_head(h, sc, qt, q, kv, kvt, dts, lses, dq0, dkv, bias0, xs, few):
    spec = pl.BlockSpec
    rows = 768 * few // HD
    apart = aligned(rows)
    tall, flat = spec((1, 512, 128), lambda s, c: (h, 0, 0)), spec((1, 128, 512), lambda s, c: (h, 0, 0))
    splits = split_shapes(apart, rows, 256)
    return pl.pallas_call(
        functools.partial(back_head_kernel, few, apart),
        out_shape=[jax.ShapeDtypeStruct((4, 3 * HD, 512), BF)] + splits,
        grid_spec=pltpu.PrefetchScalarGridSpec(
            num_scalar_prefetch=1,
            grid=(3,),
            in_specs=[flat] * 3
            + [tall] * 3
            + [tall] * 4
            + [flat] * 4
            + [spec((1, HD, 512), lambda s, c, j=j: (jnp.bitwise_xor(c[6], j), h, 0)) for j in (1, 2, 3)]
            + [spec((1, 1, 512), lambda s, c: (h, 0, 0))] * 3
            + [
                spec((1, HD, 512), lambda s, c: (h, 0, 0)),
                spec((1, 4, 512, 128), lambda s, c: (h, 0, 0, 0)),
                spec((1, HD, 1), lambda s, c: (h, 0, 0)),
            ]
            + [spec((512, 768), lambda s, c: (0, 0))] * 4,
            out_specs=[spec((4, 3 * HD, 512), lambda s, c: (0, 0, 0))]
            + [spec(v.shape, lambda s, c, d=len(v.shape): (0,) * d) for v in splits],
            scratch_shapes=[
                pltpu.VMEM((4, 512, 128), F32),
                pltpu.VMEM((4, HD, 512), BF),
                pltpu.VMEM((HD, 1), F32),
            ],
        ),
        compiler_params=params(),
        cost_estimate=LIGHT,
        name="back_head",
    )(sc, *qt[1:], *q[1:], *kv, *kvt, *[dts] * 3, *lses, dq0, dkv, bias0, *xs)


def row_mean(v):
    return jnp.mean(v, axis=1, keepdims=True)


def norm(rows):
    center = rows - row_mean(rows)
    spread = lax.rsqrt(row_mean(center * center) + EPS)
    return center * spread, spread


def norm_back(grad, normed, spread, gain):
    scaled = grad * gain
    return spread * (scaled - row_mean(scaled) - normed * row_mean(scaled * normed))


def middle_kernel(few, sc, *refs):
    m0, m1, m2, m3, x_ref, cot_ref, vec_ref, ib_ref, weights = refs[:9]
    outer = refs[9:13]
    out_ref, g1_ref, d_ref, dw_ref = refs[13:17]
    (wo_ref, n1_ref, s1_ref, hid_ref, hidb_ref, hidt_ref, acc_ref, gp_ref, act_ref, gsb_ref, gst_ref,
     dvec_ref) = refs[17:]
    step = pl.program_id(0)
    vec = lambda i: vec_ref[pl.ds(i, 1), :]
    mixed = (m0, m1, m2, m3)
    inner = lambda: weights[:, 0, :, :768].reshape(768, 768)
    outer_full = lambda: weights[:, 0, :, 768:].reshape(768, 768)
    pad = jnp.zeros((64, 512), BF)
    own_rows = 768 * few // HD

    @pl.when(step == 0)
    def _():
        for k in range(4):
            o = outer[k][:, 0].reshape(768, 768)
            wo_ref[:, k * 256 : k * 256 + 256] = jnp.concatenate(
                [o[:, h * 256 + HD : h * 256 + 2 * HD] for h in range(3)] + [jnp.zeros((768, HD), BF)], axis=1
            )
        rows = x_ref[...].astype(F32) + vec(0)
        for k in range(4):
            rows = rows + dot(mixed[k][...], wo_ref[:, k * 256 : k * 256 + 192], 0, 1)
        n1, s1 = norm(rows)
        hidden = n1 * vec(1) + vec(2)
        n1_ref[...] = n1
        s1_ref[...] = s1
        hid_ref[...] = hidden
        low = hidden.astype(BF)
        hidb_ref[...] = low
        hidt_ref[...] = low.T
        acc_ref[...] = hidden + vec(3)

    @pl.when(step < 4)
    def _():
        u = dot(hidb_ref[...], inner(), 1, 0) + ib_ref[pl.ds(step, 1), :]
        cdf = 0.5 + 0.5 * lax.erf(u * math.sqrt(0.5))
        act = (u * cdf).astype(BF)
        gp_ref[step] = cdf + u * jnp.exp(-0.5 * u * u) * (1.0 / math.sqrt(2.0 * math.pi))
        act_ref[step] = act
        acc_ref[...] += dot(act, outer_full(), 1, 1)

    @pl.when(step == 3)
    def _():
        valid = (lax.broadcasted_iota(jnp.int32, (512, 1), 0) < sc[0]).astype(F32)
        n2, s2 = norm(acc_ref[...])
        out_ref[...] = (valid * (n2 * vec(4) + vec(5))).astype(BF)
        g2 = cot_ref[...].astype(F32) * valid
        gs = norm_back(g2, n2, s2, vec(4))
        low = gs.astype(BF)
        gsb_ref[...] = low
        gst_ref[...] = low.T
        dvec_ref[pl.ds(3, 1), :] = jnp.sum(gs, axis=0, keepdims=True)
        dvec_ref[pl.ds(4, 1), :] = jnp.sum(g2 * n2, axis=0, keepdims=True)
        dvec_ref[pl.ds(5, 1), :] = jnp.sum(g2, axis=0, keepdims=True)
        acc_ref[...] = gs

    @pl.when(jnp.logical_and(step >= 4, step < 8))
    def _():
        k = 7 - step
        gi = dot(gsb_ref[...], outer_full(), 1, 0) * gp_ref[k]
        dvec_ref[pl.ds(8 + k, 1), :] = jnp.sum(gi, axis=0, keepdims=True)
        low = gi.astype(BF)
        acc_ref[...] += dot(low, inner(), 1, 1)
        at = pl.multiple_of(k * 1792, 256)
        dw_ref[:, pl.ds(at, 768)] = dot(hidt_ref[...], low, 1, 0).astype(BF)
        dw_ref[:, pl.ds(at + 768, 768)] = dot(gst_ref[...], act_ref[k], 1, 0).astype(BF)

    @pl.when(step == 8)
    def _():
        gh = acc_ref[...]
        n1 = n1_ref[...]
        g1 = norm_back(gh, n1, s1_ref[...], vec(1))
        g1_ref[...] = g1
        dvec_ref[pl.ds(0, 1), :] = jnp.sum(g1, axis=0, keepdims=True)
        dvec_ref[pl.ds(1, 1), :] = jnp.sum(gh * n1, axis=0, keepdims=True)
        dvec_ref[pl.ds(2, 1), :] = jnp.sum(gh, axis=0, keepdims=True)
        dvec_ref[pl.ds(6, 2), :] = jnp.zeros((2, 768), F32)
        dvec_ref[pl.ds(12, 4), :] = jnp.zeros((4, 768), F32)
        low = g1.astype(BF)
        lowt = low.T
        columns = dvec_ref[...].T
        lane = lax.broadcasted_iota(jnp.int32, (768, 256), 1)
        unit = lax.broadcasted_iota(jnp.int32, (768, 256), 0)
        r, l = unit_index(0), unit_index(1)
        move = (r == (l % HD) // few * own_rows + (l % HD) % few).astype(F32).astype(BF)
        shared = jnp.zeros((768, 256), F32)
        for v in range(6):
            shared = jnp.where(lane == 192 + v, columns[:, v : v + 1], shared)
        shared = shared.astype(BF).astype(F32)
        for k in range(4):
            d_ref[jnp.bitwise_xor(sc[6], k)] = dot(wo_ref[:, k * 256 : k * 256 + 192], lowt, 0, 0).astype(BF)
            full = jnp.concatenate([mixed[k][...], pad], axis=0)
            bias = jnp.where(lane - 200 == unit // HD, columns[:, 8 + k : 9 + k], 0.0).astype(BF)
            tail = dot(lowt, full, 1, 1) + shared + dot(move, bias, 1, 0)
            dw_ref[:, k * 1792 + 1536 : k * 1792 + 1792] = tail.astype(BF)


def unit_index(axis):
    return lax.broadcasted_iota(jnp.int32, (768, 768), axis)


def middle(sc, mixed, x, cot, vec, ib, weights, few):
    spec = pl.BlockSpec
    fixed = lambda shape: spec(shape, lambda i, c: (0,) * len(shape))
    once = lambda shape: spec(shape, lambda i, c: (0,) * len(shape), pipeline_mode=pl.Buffered(1))
    shape = jax.ShapeDtypeStruct
    blocks, rows = weights.shape[0], weights.shape[2]
    turn = lambda i: jnp.where(i < 4, i, jnp.where(i < 8, 7 - i, 0))
    return pl.pallas_call(
        functools.partial(middle_kernel, few),
        out_shape=[shape((512, 768), BF), shape((512, 768), F32), shape((4, 192, 512), BF)]
        + [shape((768, 7168), BF)],
        grid_spec=pltpu.PrefetchScalarGridSpec(
            num_scalar_prefetch=1,
            grid=(9,),
            in_specs=[fixed((192, 512))] * 4
            + [fixed((512, 768)), fixed((512, 768)), fixed((8, 768)), fixed((4, 768))]
            + [spec((blocks, 1, rows, 1536), lambda i, c: (0, jnp.bitwise_xor(c[6], turn(i)), 0, 0))]
            + [spec((blocks, 1, rows, 768), lambda i, c, k=k: (0, jnp.bitwise_xor(c[6], k), 0, 2)) for k in range(4)],
            out_specs=[fixed((512, 768)), fixed((512, 768)), fixed((4, 192, 512))] + [once((768, 7168))],
            scratch_shapes=[
                pltpu.VMEM((768, 1024), BF),
                pltpu.VMEM((512, 768), F32),
                pltpu.VMEM((512, 1), F32),
                pltpu.VMEM((512, 768), F32),
                pltpu.VMEM((512, 768), BF),
                pltpu.VMEM((768, 512), BF),
                pltpu.VMEM((512, 768), F32),
                pltpu.VMEM((4, 512, 768), F32),
                pltpu.VMEM((4, 512, 768), BF),
                pltpu.VMEM((512, 768), BF),
                pltpu.VMEM((768, 512), BF),
                pltpu.VMEM((16, 768), F32),
            ],
        ),
        compiler_params=params(),
        cost_estimate=LIGHT,
        name="middle",
    )(sc, *mixed, x, cot, vec, ib, *[weights] * 5)


def input_grad_kernel(heads, base_ref, w_ref, *refs):
    packets, (out, acc) = refs[:-2], refs[-2:]
    k = pl.program_id(0)

    @pl.when(k == 0)
    def _():
        acc[...] = jnp.zeros_like(acc)

    for packet, h in zip(packets, heads, strict=True):
        p = packet[0]
        p = jnp.concatenate([p[:HD], jnp.zeros((HD, 512), BF), p[HD:]], axis=0)
        acc[...] += dot(w_ref[:, 0, :, h * 256 : h * 256 + 256].reshape(768, 256), p, 1, 0)

    @pl.when(k == 3)
    def _():
        out[...] = base_ref[...] + acc[...].T


def input_grad(base, weights, packets, heads):
    blocks, _, rows, _ = weights.shape
    return pl.pallas_call(
        functools.partial(input_grad_kernel, heads),
        grid=(4,),
        out_shape=jax.ShapeDtypeStruct((512, 768), F32),
        in_specs=[whole((512, 768)), pl.BlockSpec((blocks, 1, rows, 768), lambda k: (0, k, 0, 2))]
        + [pl.BlockSpec((1, 192, 512), lambda k: (k, 0, 0))] * len(packets),
        out_specs=whole((512, 768)),
        scratch_shapes=[pltpu.VMEM((768, 512), F32)],
        compiler_params=params(),
        cost_estimate=LIGHT,
        name="input_grad",
    )(base, weights, *packets)


def body(
    tokens, cotangent, lengths, query_weight, key_weight, value_weight, query_bias, value_bias, output_weight,
    output_bias, first_gain, first_shift, inner_weight, inner_bias, outer_weight, outer_bias, second_gain, second_shift,
):
    n = lax.axis_size("dp")
    me = lax.axis_index("dp")
    rows = query_weight.shape[0]
    heads = query_weight.shape[1] // HD
    few, units = inner_bias.shape
    z = lax.axis_index("tensor")
    slots = jnp.arange(4) ^ z
    counts = jnp.clip(lengths[0] - slots * 512, 0, 512).astype(jnp.int32)
    place = jnp.stack([me & 1, me >> 1, z]).astype(jnp.int32)

    by_head = lambda w: w.reshape(rows, heads, HD)
    wide = jnp.stack(
        [by_head(query_weight), by_head(output_weight), by_head(key_weight), by_head(value_weight)], axis=2
    ).reshape(rows, heads * 256)
    small = jnp.stack([output_bias, first_gain, first_shift, outer_bias, second_gain, second_shift], axis=1)
    inner_bias = exchange(jnp.broadcast_to(inner_bias[None], (4, few, units)))
    biases = jnp.concatenate([query_bias, value_bias] + [pick(inner_bias, z ^ k) for k in range(4)], axis=1)
    used = 6 + biases.shape[1]
    biases = jnp.pad(biases, ((0, rows - few), (0, 0)))
    near = jnp.concatenate([wide, small, biases, jnp.zeros((rows, 128 - used), BF)], axis=1)

    every = jnp.concatenate([inner_weight, outer_weight, wide], axis=1)
    apart = aligned(rows)
    also = lambda a, m: jnp.concatenate([a, swap(a, "dp", m)], axis=0) if apart else a
    up, down = [tokens], [tokens]

    def hop():
        up.append(shift(up[-1], 1))
        down.append(shift(down[-1], -1))

    hop()
    near = also(near, 2)
    near, up[1], down[1], every = stage(near, up[1], down[1], every)
    every = gather_all(every)
    hop()
    near = also(near, 4)
    near, up[2], down[2] = stage(near, up[2], down[2])
    hop()
    if apart:
        at = [me ^ m for m in (0, 2, 4, 6, 1, 3, 5, 7)]
        near, where = [near, swap(near, "dp", 1)], jnp.stack(at).astype(jnp.int32) * rows
    else:
        near, where = [gather_rows(near)], jnp.zeros((1,), jnp.int32)
    tile = assemble(near, where, 128, 6).astype(F32)
    vec = jnp.pad(tile[:, :6].T, ((0, 2), (0, 0)))
    tile = tile.reshape(n, rows, 128)[:, :few, 6:used].reshape(HD, used - 6).T
    blank = jnp.zeros((heads, 2 * HD), F32)
    bias = jnp.concatenate([tile[:heads], blank, tile[heads : 2 * heads]], axis=1)[:, None, :]
    ib = tile[2 * heads :].reshape(4, units * HD)
    xs = [by_slot(up, down, k) for k in range(3)]
    made = [project(x, (near, where), bias) for x in xs]
    made, up[3], down[3] = stage(made, up[3], down[3])
    xs.append(by_slot(up, down, 3))
    made.append(project(xs[3], (near, where), bias))
    qt, q, kv, kvt = ([m[i] for m in made] for i in range(4))

    mixed, lses = [None] * 4, [None] * 4
    for s in (3, 2, 1, 0):
        mixed[s], lses[s] = attend(counts, qt[s], kv, kvt)
        if s:
            come = mixed[s + 1] if s < 3 else ()
            mixed[s], qt[s - 1], come = stage(mixed[s], qt[s - 1], come)
            if s < 3:
                mixed[s + 1] = come
            mixed[s] = swap(mixed[s], "tensor", s)
    mixed, every = stage(mixed, every)

    sc = jnp.concatenate([counts, place])
    out, g1, d_out, dw = middle(sc, mixed, tokens, cotangent, vec, ib, every, few)

    total = lax.psum_scatter(dw, "dp", scatter_dimension=0, tiled=True)
    d = exchange(d_out)
    dq0, dkv, bias0 = back_own(sc, qt[0], q[0], kv, kvt, d_out, lses[0])
    d, dq0, dkv, bias0 = stage(d, dq0, dkv, bias0)
    head = lambda h, d: back_head(h, sc, qt, q, kv, kvt, d, lses[1:], dq0, dkv, bias0, xs, few)
    packet0, *dw0 = head(0, d)
    packet0, dw0, d = stage(packet0, dw0, d)
    packet0 = exchange(packet0)
    packet1, *dw1 = head(1, d)
    packet0, packet1, dw1, d = stage(packet0, packet1, dw1, d)
    packet1 = exchange(packet1)
    packet2, *dw2 = head(2, d)
    packet1, packet2, dw2, total = stage(packet1, packet2, dw2, total)

    packet2 = exchange(packet2)
    dws = [dw0, dw1, dw2]
    joined = lambda arrays: jnp.concatenate(arrays, axis=-1)
    if apart:
        own_keep, own_got = joined([v[0] for v in dws]), swap(joined([v[1] for v in dws]), "dp", 1)
    else:
        own_keep = own_got = joined([v[0] for v in dws])
    slots = [total[:, k * 1792 : k * 1792 + 1792] for k in range(4)]
    moved = [swap(v, "tensor", k) for k, v in enumerate(slots) if k]
    ahead = input_grad(g1, every, [packet0, packet1], (0, 1))
    packet2, ahead, own_keep, own_got = stage(packet2, ahead, own_keep, own_got)
    tokens_grad = input_grad(ahead, every, [packet2], (2,))
    if apart:
        block = lambda m: own_keep[m].astype(F32) + own_got[m].astype(F32)
        passed = swap(jnp.stack([block(1), block(3)]).astype(BF), "dp", 2)
        near_by = (block(2) + passed[1].astype(F32)).astype(BF)
        own = block(0) + passed[0].astype(F32) + swap(near_by, "dp", 4).astype(F32)
    else:
        own = sum_rows(own_keep)

    sums = (slots[0].astype(F32) + moved[0].astype(F32)) + (moved[1].astype(F32) + moved[2].astype(F32))
    ffn, rest = sums[:, :1536], sums[:, 1536:]
    side = lambda i: jnp.concatenate([own[:, h * 256 + i * HD : h * 256 + i * HD + HD] for h in range(heads)], axis=1)
    return (
        out,
        tokens_grad,
        side(0),
        side(1),
        side(2),
        jnp.stack([own[:few, h * 256 + 192] for h in range(heads)], axis=1),
        jnp.stack([own[:few, h * 256 + 193] for h in range(heads)], axis=1),
        rest[:, :192],
        rest[:, 192],
        rest[:, 193],
        rest[:, 194],
        ffn[:, :768],
        rest[:few, 200 : 200 + units],
        ffn[:, 768:],
        rest[:, 195],
        rest[:, 196],
        rest[:, 197],
    )


def solution(mesh):
    table, vector, token = P("dp", "tensor"), P("dp"), P(("dp", "tensor"), None)
    return jax.shard_map(
        body,
        mesh=mesh,
        in_specs=(
            token, token, vector, table, table, table, table, table, table,
            vector, vector, vector, table, table, table, vector, vector, vector,
        ),
        out_specs=(
            token, token, table, table, table, table, table, table,
            vector, vector, vector, table, table, table, vector, vector, vector,
        ),
        check_vma=False,
    )
```

profile of v0, /device:TPU:0, one launch (start us, length us, event | category | flops | bytes accessed | tf_op | source)
XLA Modules:
  0.0 382.4 jit_solution(12761719870168611516)
XLA Ops:
  8.6 5.6 %collective-permute-start.1 = (bf16[512,768]{1,0:T(8,128)(2,1)}, bf16[512,768]{1,0:T(8,128)(2,1)S(1)}, u32[]{:S(2)}, u32[]{:S(2)}) collective-permute-start(bf16[512,768]{1,0:T(8,128)(2,1)} %refs_23_.5), channel_id=1, source_target_pairs={{0,1},{1,2},{2,3},{4,5},{5,6},{6,7},{8,9},{9,10},{10,11},{12,13},{... | collective-permute-start | bytes 2359304 | tf_op jit(solution)/shard_map/ppermute | solution.py:56
  45.8 5.6 %collective-permute-done.3 = bf16[192,896]{1,0:T(8,128)(2,1)S(1)} collective-permute-done((bf16[192,896]{1,0:T(8,128)(2,1)S(1)}, bf16[192,896]{1,0:T(8,128)(2,1)S(1)}, u32[]{:S(2)}, u32[]{:S(2)}) %collective-permute-start.3) | collective-permute-done | bytes 344096 | tf_op jit(solution)/shard_map/ppermute | solution.py:35
  51.5 15.3 %collective-permute-done.4 = bf16[512,768]{1,0:T(8,128)(2,1)S(1)} collective-permute-done((bf16[512,768]{1,0:T(8,128)(2,1)S(1)}, bf16[512,768]{1,0:T(8,128)(2,1)S(1)}, u32[]{:S(2)}, u32[]{:S(2)}) %collective-permute-start.4) | collective-permute-done | bytes 786464 | tf_op jit(solution)/shard_map/ppermute | solution.py:56
  86.1 4.9 %project.4 = (bf16[3,128,512]{2,1,0:T(8,128)(2,1)}, bf16[3,512,128]{2,1,0:T(8,128)(2,1)}, bf16[3,512,128]{2,1,0:T(8,128)(2,1)}, bf16[3,128,512]{2,1,0:T(8,128)(2,1)}) custom-call(s32[8]{0:T(128)} %broadcast_multiply_fusion.where, bf16[512,768]{1,0:T(8,128)(2,1)} %refs_23_.5, f32[3,1,256]{2,1,0:T(1,128)} %broadcast_in_dim.18.b_ref, ...), custom_call_target="tpu_custom_call" | custom-call | flops 1 | bytes 1 | tf_op jit(solution)/shard_map/project/pallas_call | solution.py:234
  95.9 4.9 %project.5 = (bf16[3,128,512]{2,1,0:T(8,128)(2,1)}, bf16[3,512,128]{2,1,0:T(8,128)(2,1)}, bf16[3,512,128]{2,1,0:T(8,128)(2,1)}, bf16[3,128,512]{2,1,0:T(8,128)(2,1)}) custom-call(s32[8]{0:T(128)} %broadcast_multiply_fusion.where, bf16[512,768]{1,0:T(8,128)(2,1)} %broadcast_select_fusion.1.x_ref.refs_24_, f32[3,1,256]{2,1,0:T(1,128)} %broadcast_in_dim.18.b_ref, ...), custom_call_target="tpu_custom_call" | custom-call | flops 1 | bytes 1 | tf_op jit(solution)/shard_map/project/pallas_call | solution.py:234
  100.8 9.5 %collective-permute-done.7 = bf16[512,768]{1,0:T(8,128)(2,1)} collective-permute-done((bf16[512,768]{1,0:T(8,128)(2,1)S(1)}, bf16[512,768]{1,0:T(8,128)(2,1)}, u32[]{:S(2)}, u32[]{:S(2)}) %collective-permute-start.7) | collective-permute-done | bytes 786464 | tf_op jit(solution)/shard_map/ppermute | solution.py:56
  115.8 5.2 %project.7 = (bf16[3,128,512]{2,1,0:T(8,128)(2,1)}, bf16[3,512,128]{2,1,0:T(8,128)(2,1)}, bf16[3,512,128]{2,1,0:T(8,128)(2,1)}, bf16[3,128,512]{2,1,0:T(8,128)(2,1)}) custom-call(s32[8]{0:T(128)} %broadcast_multiply_fusion.where, bf16[512,768]{1,0:T(8,128)(2,1)} %select_select_fusion.x_ref.refs_26_, f32[3,1,256]{2,1,0:T(1,128)} %broadcast_in_dim.18.b_ref, ...), custom_call_target="tpu_custom_call" | custom-call | flops 1 | bytes 1 | tf_op jit(solution)/shard_map/project/pallas_call | solution.py:234
  121.0 8.5 %attend.4 = (bf16[192,512]{1,0:T(8,128)(2,1)}, f32[3,1,512]{2,1,0:T(1,128)}) custom-call(s32[4]{0:T(128)} %subtract_clamp_fusion.counts, bf16[3,128,512]{2,1,0:T(8,128)(2,1)} %get-tuple-element.133.qt_ref.refs_2_, bf16[3,512,128]{2,1,0:T(8,128)(2,1)} %get-tuple-element.134.k0.refs_0_.refs_6_, bf16[3,512,128]{2,1,0:T(8,128)(2,1)} %get-tuple-element.135.k1.refs_1_.refs_7_, ...), custom_call_target="tpu_custom_call" | custom-call | flops 1 | bytes 1 | tf_op jit(solution)/shard_map/attend/pallas_call | solution.py:273
  131.7 8.5 %attend.5 = (bf16[192,512]{1,0:T(8,128)(2,1)}, f32[3,1,512]{2,1,0:T(1,128)}) custom-call(s32[4]{0:T(128)} %subtract_clamp_fusion.counts, bf16[3,128,512]{2,1,0:T(8,128)(2,1)} %get-tuple-element.144.qt_ref.refs_1_, bf16[3,512,128]{2,1,0:T(8,128)(2,1)} %get-tuple-element.134.k0.refs_0_.refs_6_, bf16[3,512,128]{2,1,0:T(8,128)(2,1)} %get-tuple-element.135.k1.refs_1_.refs_7_, ...), custom_call_target="tpu_custom_call" | custom-call | flops 1 | bytes 1 | tf_op jit(solution)/shard_map/attend/pallas_call | solution.py:273
  143.3 13.5 %collective-permute-start.10 = (bf16[192,512]{1,0:T(8,128)(2,1)}, bf16[192,512]{1,0:T(8,128)(2,1)S(1)}, u32[]{:S(2)}, u32[]{:S(2)}) collective-permute-start(bf16[192,512]{1,0:T(8,128)(2,1)} %get-tuple-element.151), channel_id=1, source_target_pairs={{0,2},{1,3},{2,0},{3,1},{4,6},{5,7},{6,4},{7,5},{8,10},{9,11},{10,... | collective-permute-start | bytes 589832 | tf_op jit(solution)/shard_map/ppermute | solution.py:35
  158.1 8.5 %attend.6 = (bf16[192,512]{1,0:T(8,128)(2,1)}, f32[3,1,512]{2,1,0:T(1,128)}) custom-call(s32[4]{0:T(128)} %subtract_clamp_fusion.counts, bf16[3,128,512]{2,1,0:T(8,128)(2,1)} %get-tuple-element.148.qt_ref.refs_0_, bf16[3,512,128]{2,1,0:T(8,128)(2,1)} %get-tuple-element.134.k0.refs_0_.refs_6_, bf16[3,512,128]{2,1,0:T(8,128)(2,1)} %get-tuple-element.135.k1.refs_1_.refs_7_, ...), custom_call_target="tpu_custom_call" | custom-call | flops 1 | bytes 1 | tf_op jit(solution)/shard_map/attend/pallas_call | solution.py:273
  166.6 7.4 %collective-permute-done.10.refs_2_ = bf16[192,512]{1,0:T(8,128)(2,1)S(1)} collective-permute-done((bf16[192,512]{1,0:T(8,128)(2,1)}, bf16[192,512]{1,0:T(8,128)(2,1)S(1)}, u32[]{:S(2)}, u32[]{:S(2)}) %collective-permute-start.10) | collective-permute-done | bytes 196640 | tf_op jit(solution)/shard_map/ppermute | solution.py:35
  174.7 8.7 %attend.7 = (bf16[192,512]{1,0:T(8,128)(2,1)}, f32[3,1,512]{2,1,0:T(1,128)}) custom-call(s32[4]{0:T(128)} %subtract_clamp_fusion.counts, bf16[3,128,512]{2,1,0:T(8,128)(2,1)} %get-tuple-element.152.qt_ref, bf16[3,512,128]{2,1,0:T(8,128)(2,1)} %get-tuple-element.134.k0.refs_0_.refs_6_, bf16[3,512,128]{2,1,0:T(8,128)(2,1)} %get-tuple-element.135.k1.refs_1_.refs_7_, ...), custom_call_target="tpu_custom_call" | custom-call | flops 1 | bytes 1 | tf_op jit(solution)/shard_map/attend/pallas_call | solution.py:273
  184.1 36.3 %middle.1 = (bf16[512,768]{1,0:T(8,128)(2,1)}, f32[512,768]{1,0:T(8,128)}, bf16[4,192,512]{2,1,0:T(8,128)(2,1)}, bf16[768,7168]{1,0:T(8,128)(2,1)}) custom-call(s32[7]{0:T(128)} %pad_add_fusion.sc.counts, bf16[192,512]{1,0:T(8,128)(2,1)} %get-tuple-element.158.refs_0_, bf16[192,512]{1,0:T(8,128)(2,1)} %copy-done.15, bf16[192,512]{1,0:T(8,128)(2,1)} %copy-done.14, ...), custom_call_target="tpu_custom_call" | custom-call | flops 1 | bytes 1 | tf_op jit(solution)/shard_map/middle/pallas_call | solution.py:557
  224.3 13.3 %back_own.1 = (bf16[3,64,512]{2,1,0:T(8,128)(2,1)}, f32[3,4,512,128]{3,2,1,0:T(8,128)}, f32[3,64,1]{2,1,0:T(8,128)}) custom-call(s32[7]{0:T(128)} %pad_add_fusion.sc.counts, bf16[3,128,512]{2,1,0:T(8,128)(2,1)} %get-tuple-element.152.qt_ref, bf16[3,512,128]{2,1,0:T(8,128)(2,1)} %get-tuple-element.168.q_ref, ...), custom_call_target="tpu_custom_call" | custom-call | flops 1 | bytes 1 | tf_op jit(solution)/shard_map/back_own/pallas_call | solution.py:326
  237.6 7.1 %all-to-all-done.1.refs_14_.refs_15_.refs_16_ = bf16[4,192,512]{2,1,0:T(8,128)(2,1)S(1)} async-done(((bf16[4,192,512]{2,1,0:T(8,128)(2,1)}), bf16[4,192,512]{2,1,0:T(8,128)(2,1)S(1)}, u32[]{:S(2)}, u32[]{:S(2)}) %all-to-all-start.1) | async-done | bytes 786464 | tf_op jit(solution)/shard_map/all_to_all | solution.py:72
  245.5 16.1 %back_head.3 = (bf16[4,192,512]{2,1,0:T(8,128)(2,1)}, bf16[4,96,256]{2,1,0:T(8,128)(2,1)}, bf16[4,96,256]{2,1,0:T(8,128)(2,1)}) custom-call(s32[7]{0:T(128)} %pad_add_fusion.sc.counts, bf16[3,128,512]{2,1,0:T(8,128)(2,1)} %get-tuple-element.148.qt_ref.refs_0_, bf16[3,128,512]{2,1,0:T(8,128)(2,1)} %get-tuple-element.144.qt_ref.refs_1_, ...), custom_call_target="tpu_custom_call" | custom-call | flops 1 | bytes 1 | tf_op jit(solution)/shard_map/back_head/pallas_call | solution.py:400
  265.4 15.8 %back_head.4 = (bf16[4,192,512]{2,1,0:T(8,128)(2,1)}, bf16[4,96,256]{2,1,0:T(8,128)(2,1)}, bf16[4,96,256]{2,1,0:T(8,128)(2,1)}) custom-call(s32[7]{0:T(128)} %pad_add_fusion.sc.counts, bf16[3,128,512]{2,1,0:T(8,128)(2,1)} %get-tuple-element.148.qt_ref.refs_0_, bf16[3,128,512]{2,1,0:T(8,128)(2,1)} %get-tuple-element.144.qt_ref.refs_1_, ...), custom_call_target="tpu_custom_call" | custom-call | flops 1 | bytes 1 | tf_op jit(solution)/shard_map/back_head/pallas_call | solution.py:400
  288.9 15.8 %back_head.5 = (bf16[4,192,512]{2,1,0:T(8,128)(2,1)}, bf16[4,96,256]{2,1,0:T(8,128)(2,1)}, bf16[4,96,256]{2,1,0:T(8,128)(2,1)}) custom-call(s32[7]{0:T(128)} %pad_add_fusion.sc.counts, bf16[3,128,512]{2,1,0:T(8,128)(2,1)} %get-tuple-element.148.qt_ref.refs_0_, bf16[3,128,512]{2,1,0:T(8,128)(2,1)} %get-tuple-element.144.qt_ref.refs_1_, ...), custom_call_target="tpu_custom_call" | custom-call | flops 1 | bytes 1 | tf_op jit(solution)/shard_map/back_head/pallas_call | solution.py:400
  318.7 6.9 %input_grad.2.base_ref = f32[512,768]{1,0:T(8,128)} custom-call(f32[512,768]{1,0:T(8,128)} %get-tuple-element.195.base_ref, bf16[8,4,96,2304]{3,2,1,0:T(8,128)(2,1)} %bitcast.48, bf16[4,192,512]{2,1,0:T(8,128)(2,1)} %copy-done.4, bf16[4,192,512]{2,1,0:T(8,128)(2,1)} %copy-done.5), custom_call_target="tpu_custom_call" | custom-call | flops 1 | bytes 1 | tf_op jit(solution)/shard_map/input_grad/pallas_call | solution.py:610
  325.7 7.3 %all-to-all-done.4.refs_0_ = bf16[4,192,512]{2,1,0:T(8,128)(2,1)S(1)} async-done(((bf16[4,192,512]{2,1,0:T(8,128)(2,1)}), bf16[4,192,512]{2,1,0:T(8,128)(2,1)S(1)}, u32[]{:S(2)}, u32[]{:S(2)}) %all-to-all-start.4) | async-done | bytes 786464 | tf_op jit(solution)/shard_map/all_to_all | solution.py:72
  334.4 11.2 %collective-permute-done.17 = bf16[96,1792]{1,0:T(8,128)(2,1)} collective-permute-done((bf16[96,1792]{1,0:T(8,128)(2,1)}, bf16[96,1792]{1,0:T(8,128)(2,1)}, u32[]{:S(2)}, u32[]{:S(2)}) %collective-permute-start.17) | collective-permute-done | bytes 344096 | tf_op jit(solution)/shard_map/ppermute | solution.py:35
  345.5 16.0 %collective-permute-done.16 = bf16[96,1792]{1,0:T(8,128)(2,1)} collective-permute-done((bf16[96,1792]{1,0:T(8,128)(2,1)}, bf16[96,1792]{1,0:T(8,128)(2,1)}, u32[]{:S(2)}, u32[]{:S(2)}) %collective-permute-start.16) | collective-permute-done | bytes 344096 | tf_op jit(solution)/shard_map/ppermute | solution.py:35
  366.0 6.1 %input_grad.3 = f32[512,768]{1,0:T(8,128)} custom-call(f32[512,768]{1,0:T(8,128)} %input_grad.2.base_ref, bf16[8,4,96,2304]{3,2,1,0:T(8,128)(2,1)} %bitcast.49, bf16[4,192,512]{2,1,0:T(8,128)(2,1)} %copy-done.3), custom_call_target="tpu_custom_call" | custom-call | flops 1 | bytes 1 | tf_op jit(solution)/shard_map/input_grad/pallas_call | solution.py:610
  (149 shorter events, 109.1 us)
Async XLA Ops:
  7.2 30.9 %collective-permute-start.2 = (bf16[512,768]{1,0:T(8,128)(2,1)}, bf16[512,768]{1,0:T(8,128)(2,1)S(1)}, u32[]{:S(2)}, u32[]{:S(2)}) collective-permute-start(bf16[512,768]{1,0:T(8,128)(2,1)} %refs_23_.5), channel_id=1, source_target_pairs={{1,0},{2,1},{3,2},{5,4},{6,5},{7,6},{9,8},{10,9},{11,10},{13,12},{... | collective-permute-start | bytes 2359304 | tf_op jit(solution)/shard_map/ppermute | solution.py:56
  8.6 29.4 %collective-permute-start.1 = (bf16[512,768]{1,0:T(8,128)(2,1)}, bf16[512,768]{1,0:T(8,128)(2,1)S(1)}, u32[]{:S(2)}, u32[]{:S(2)}) collective-permute-start(bf16[512,768]{1,0:T(8,128)(2,1)} %refs_23_.5), channel_id=1, source_target_pairs={{0,1},{1,2},{2,3},{4,5},{5,6},{6,7},{8,9},{9,10},{10,11},{12,13},{... | collective-permute-start | bytes 2359304 | tf_op jit(solution)/shard_map/ppermute | solution.py:56
  15.5 16.7 %all-to-all-start = ((bf16[4,8,12]{2,1,0:T(8,128)(2,1)}), bf16[4,8,12]{2,1,0:T(8,128)(2,1)S(1)}, u32[]{:S(2)}, u32[]{:S(2)}) async-start(bf16[4,8,12]{2,1,0:T(8,128)(2,1)} %broadcast_in_dim.15), calls=%async_computation | async-start | bytes 16384 | tf_op jit(solution)/shard_map/all_to_all | solution.py:72
  19.8 163.6 %all-gather.3.cloned.1.call-start = ((), (), s32[]{:S(2)}) async-start(), calls=%async_computation.7 | async-start | bytes 14598144 | tf_op jit(solution)/shard_map/all_gather | solution.py:82
  39.1 269.4 %reduce-scatter.2.cloned.1.call-start = ((), (), s32[]{:S(2)}) async-start(), calls=%async_computation.6 | async-start | bytes 12386304 | tf_op jit(solution)/shard_map/reduce_scatter | solution.py:698
  39.2 27.6 %collective-permute-start.4 = (bf16[512,768]{1,0:T(8,128)(2,1)S(1)}, bf16[512,768]{1,0:T(8,128)(2,1)S(1)}, u32[]{:S(2)}, u32[]{:S(2)}) collective-permute-start(bf16[512,768]{1,0:T(8,128)(2,1)S(1)} %collective-permute-done.1), channel_id=1, source_target_pairs={{0,1},{1,2},{2,3},{4,5},{5,6},{6,7},{8,9},{9,10},{10,11},{12,13},{... | collective-permute-start | bytes 2359304 | tf_op jit(solution)/shard_map/ppermute | solution.py:56
  42.6 28.4 %collective-permute-start.5 = (bf16[512,768]{1,0:T(8,128)(2,1)S(1)}, bf16[512,768]{1,0:T(8,128)(2,1)}, u32[]{:S(2)}, u32[]{:S(2)}) collective-permute-start(bf16[512,768]{1,0:T(8,128)(2,1)S(1)} %collective-permute-done.2), channel_id=1, source_target_pairs={{1,0},{2,1},{3,2},{5,4},{6,5},{7,6},{9,8},{10,9},{11,10},{13,12},{... | collective-permute-start | bytes 2359304 | tf_op jit(solution)/shard_map/ppermute | solution.py:56
  43.9 7.5 %collective-permute-start.3 = (bf16[192,896]{1,0:T(8,128)(2,1)S(1)}, bf16[192,896]{1,0:T(8,128)(2,1)S(1)}, u32[]{:S(2)}, u32[]{:S(2)}) collective-permute-start(bf16[192,896]{1,0:T(8,128)(2,1)S(1)} %pad_maximum_fusion.4), channel_id=1, source_target_pairs={{0,16},{4,20},{8,24},{12,28},{16,0},{20,4},{24,8},{28,12},{1,17},{... | collective-permute-start | bytes 1032200 | tf_op jit(solution)/shard_map/ppermute | solution.py:35
  71.0 9.2 %collective-permute-start.6 = (bf16[384,896]{1,0:T(8,128)(2,1)S(1)}, bf16[384,896]{1,0:T(8,128)(2,1)S(1)}, u32[]{:S(2)}, u32[]{:S(2)}) collective-permute-start(bf16[384,896]{1,0:T(8,128)(2,1)S(1)} %pad_maximum_fusion.refs_0_), channel_id=1, source_target_pairs={{0,4},{4,0},{8,12},{12,8},{16,20},{20,16},{24,28},{28,24},{1,5},{5... | collective-permute-start | bytes 2064392 | tf_op jit(solution)/shard_map/ppermute | solution.py:35
  72.5 37.8 %collective-permute-start.7 = (bf16[512,768]{1,0:T(8,128)(2,1)S(1)}, bf16[512,768]{1,0:T(8,128)(2,1)}, u32[]{:S(2)}, u32[]{:S(2)}) collective-permute-start(bf16[512,768]{1,0:T(8,128)(2,1)S(1)} %collective-permute-done.4), channel_id=1, source_target_pairs={{0,1},{1,2},{2,3},{4,5},{5,6},{6,7},{8,9},{9,10},{10,11},{12,13},{... | collective-permute-start | bytes 2359304 | tf_op jit(solution)/shard_map/ppermute | solution.py:56
  76.7 36.5 %collective-permute-start.8 = (bf16[512,768]{1,0:T(8,128)(2,1)}, bf16[512,768]{1,0:T(8,128)(2,1)}, u32[]{:S(2)}, u32[]{:S(2)}) collective-permute-start(bf16[512,768]{1,0:T(8,128)(2,1)} %collective-permute-done.5), channel_id=1, source_target_pairs={{1,0},{2,1},{3,2},{5,4},{6,5},{7,6},{9,8},{10,9},{11,10},{13,12},{... | collective-permute-start | bytes 2359304 | tf_op jit(solution)/shard_map/ppermute | solution.py:56
  129.6 13.7 %collective-permute-start.9 = (bf16[192,512]{1,0:T(8,128)(2,1)}, bf16[192,512]{1,0:T(8,128)(2,1)S(1)}, u32[]{:S(2)}, u32[]{:S(2)}) collective-permute-start(bf16[192,512]{1,0:T(8,128)(2,1)} %get-tuple-element.147), channel_id=1, source_target_pairs={{0,3},{1,2},{2,1},{3,0},{4,7},{5,6},{6,5},{7,4},{8,11},{9,10},{10,... | collective-permute-start | bytes 589832 | tf_op jit(solution)/shard_map/ppermute | solution.py:35
  143.3 30.7 %collective-permute-start.10 = (bf16[192,512]{1,0:T(8,128)(2,1)}, bf16[192,512]{1,0:T(8,128)(2,1)S(1)}, u32[]{:S(2)}, u32[]{:S(2)}) collective-permute-start(bf16[192,512]{1,0:T(8,128)(2,1)} %get-tuple-element.151), channel_id=1, source_target_pairs={{0,2},{1,3},{2,0},{3,1},{4,6},{5,7},{6,4},{7,5},{8,10},{9,11},{10,... | collective-permute-start | bytes 589832 | tf_op jit(solution)/shard_map/ppermute | solution.py:35
  174.0 9.4 %collective-permute-start.11 = (bf16[192,512]{1,0:T(8,128)(2,1)}, bf16[192,512]{1,0:T(8,128)(2,1)S(1)}, u32[]{:S(2)}, u32[]{:S(2)}) collective-permute-start(bf16[192,512]{1,0:T(8,128)(2,1)} %get-tuple-element.154), channel_id=1, source_target_pairs={{0,1},{1,0},{2,3},{3,2},{4,5},{5,4},{6,7},{7,6},{8,9},{9,8},{10,11... | collective-permute-start | bytes 589832 | tf_op jit(solution)/shard_map/ppermute | solution.py:35
  220.4 24.3 %all-to-all-start.1 = ((bf16[4,192,512]{2,1,0:T(8,128)(2,1)}), bf16[4,192,512]{2,1,0:T(8,128)(2,1)S(1)}, u32[]{:S(2)}, u32[]{:S(2)}) async-start(bf16[4,192,512]{2,1,0:T(8,128)(2,1)} %get-tuple-element.167.refs_8_), calls=%async_computation.1 | async-start | bytes 1572864 | tf_op jit(solution)/shard_map/all_to_all | solution.py:72
  261.7 23.7 %all-to-all-start.2 = ((bf16[4,192,512]{2,1,0:T(8,128)(2,1)}), bf16[4,192,512]{2,1,0:T(8,128)(2,1)S(1)}, u32[]{:S(2)}, u32[]{:S(2)}) async-start(bf16[4,192,512]{2,1,0:T(8,128)(2,1)} %get-tuple-element.183), calls=%async_computation.2 | async-start | bytes 1572864 | tf_op jit(solution)/shard_map/all_to_all | solution.py:72
  285.4 23.1 %all-to-all-start.3 = ((bf16[4,192,512]{2,1,0:T(8,128)(2,1)}), bf16[4,192,512]{2,1,0:T(8,128)(2,1)S(1)}, u32[]{:S(2)}, u32[]{:S(2)}) async-start(bf16[4,192,512]{2,1,0:T(8,128)(2,1)} %get-tuple-element.188), calls=%async_computation.3 | async-start | bytes 1572864 | tf_op jit(solution)/shard_map/all_to_all | solution.py:72
  308.5 24.5 %all-to-all-start.4 = ((bf16[4,192,512]{2,1,0:T(8,128)(2,1)}), bf16[4,192,512]{2,1,0:T(8,128)(2,1)S(1)}, u32[]{:S(2)}, u32[]{:S(2)}) async-start(bf16[4,192,512]{2,1,0:T(8,128)(2,1)} %get-tuple-element.194), calls=%async_computation.5 | async-start | bytes 1572864 | tf_op jit(solution)/shard_map/all_to_all | solution.py:72
  313.3 12.4 %collective-permute-start.12 = (bf16[4,96,768]{2,1,0:T(8,128)(2,1)}, bf16[4,96,768]{2,1,0:T(8,128)(2,1)S(1)}, u32[]{:S(2)}, u32[]{:S(2)}) collective-permute-start(bf16[4,96,768]{2,1,0:T(8,128)(2,1)} %pad_maximum_fusion.3), channel_id=1, source_target_pairs={{0,4},{4,0},{8,12},{12,8},{16,20},{20,16},{24,28},{28,24},{1,5},{5... | collective-permute-start | bytes 1769480 | tf_op jit(solution)/shard_map/ppermute | solution.py:35
  314.3 20.1 %collective-permute-start.15 = (bf16[96,1792]{1,0:T(8,128)(2,1)}, bf16[96,1792]{1,0:T(8,128)(2,1)}, u32[]{:S(2)}, u32[]{:S(2)}) collective-permute-start(bf16[96,1792]{1,0:T(8,128)(2,1)} %get-tuple-element.266), channel_id=1, source_target_pairs={{0,1},{1,0},{2,3},{3,2},{4,5},{5,4},{6,7},{7,6},{8,9},{9,8},{10,11... | collective-permute-start | bytes 1032200 | tf_op jit(solution)/shard_map/ppermute | solution.py:35
  316.3 29.3 %collective-permute-start.17 = (bf16[96,1792]{1,0:T(8,128)(2,1)}, bf16[96,1792]{1,0:T(8,128)(2,1)}, u32[]{:S(2)}, u32[]{:S(2)}) collective-permute-start(bf16[96,1792]{1,0:T(8,128)(2,1)} %get-tuple-element.267), channel_id=1, source_target_pairs={{0,3},{1,2},{2,1},{3,0},{4,7},{5,6},{6,5},{7,4},{8,11},{9,10},{10,... | collective-permute-start | bytes 1032200 | tf_op jit(solution)/shard_map/ppermute | solution.py:35
  318.7 42.9 %collective-permute-start.16 = (bf16[96,1792]{1,0:T(8,128)(2,1)}, bf16[96,1792]{1,0:T(8,128)(2,1)}, u32[]{:S(2)}, u32[]{:S(2)}) collective-permute-start(bf16[96,1792]{1,0:T(8,128)(2,1)} %get-tuple-element.268), channel_id=1, source_target_pairs={{0,2},{1,3},{2,0},{3,1},{4,6},{5,7},{6,4},{7,5},{8,10},{9,11},{10,... | collective-permute-start | bytes 1032200 | tf_op jit(solution)/shard_map/ppermute | solution.py:35
  333.1 29.8 %collective-permute-start.13 = (bf16[2,96,768]{2,1,0:T(8,128)(2,1)S(1)}, bf16[2,96,768]{2,1,0:T(8,128)(2,1)S(1)}, u32[]{:S(2)}, u32[]{:S(2)}) collective-permute-start(bf16[2,96,768]{2,1,0:T(8,128)(2,1)S(1)} %pad_maximum_fusion.5), channel_id=1, source_target_pairs={{0,8},{4,12},{8,0},{12,4},{16,24},{20,28},{24,16},{28,20},{1,9},{5... | collective-permute-start | bytes 884744 | tf_op jit(solution)/shard_map/ppermute | solution.py:35
  363.0 9.2 %collective-permute-start.14 = (bf16[96,768]{1,0:T(8,128)(2,1)S(1)}, bf16[96,768]{1,0:T(8,128)(2,1)S(1)}, u32[]{:S(2)}, u32[]{:S(2)}) collective-permute-start(bf16[96,768]{1,0:T(8,128)(2,1)S(1)} %fusion), channel_id=1, source_target_pairs={{0,16},{4,20},{8,24},{12,28},{16,0},{20,4},{24,8},{28,12},{1,17},{... | collective-permute-start | bytes 442376 | tf_op jit(solution)/shard_map/ppermute | solution.py:35
  (20 other events, 237.0 us)
Sparse Core Ops, SparseCore 0:
  39.2 139.6 all-gather.2
  220.5 83.1 reduce-scatter.1
where the time goes:
time: 387 us; the launch traced here: 382 us
  Pallas kernels  167 us (43%)
  waiting for transfers between devices  105 us (27%)
  starting transfers between devices  60.1 us (16%)
  local copies, waits for them, and re-layouts  24.2 us (6%)
  between operations  15.4 us (4%)
  other arithmetic  11.3 us (3%)
    ppermute x12, waiting for transfers between devices, swap(): return lax.ppermute(x, axis, [(i, i ^ mask) for i in range(n)])  48.2 us
    pallas_call x3, Pallas kernels, back_head(): pl.pallas_call(functools.partial(back_head_kernel, few, apart), out_shape...  47.7 us
    pallas_call x1, Pallas kernels, middle(): pl.pallas_call(functools.partial(middle_kernel, few), out_shape=[shape((5...  36.3 us
    pallas_call x4, Pallas kernels, attend(): pl.pallas_call(attend_kernel, out_shape=[jax.ShapeDtypeStruct((heads * HD...  34.2 us
    ppermute x6, waiting for transfers between devices, shift(): lax.ppermute(x, 'tensor', [(i, i + by) for i in range(n) if 0 <= i + by <...  31.8 us
    all_to_all x5, waiting for transfers between devices, exchange(): return lax.all_to_all(blocks, 'tensor', 0, 0)  24.4 us
    ppermute x12, starting transfers between devices, swap(): return lax.ppermute(x, axis, [(i, i ^ mask) for i in range(n)])  23.5 us
    pallas_call x4, Pallas kernels, project(): pl.pallas_call(project_kernel, out_shape=[jax.ShapeDtypeStruct(s, BF) for...  19.9 us
  transfers between devices with their start and end apart: 25, of which 16 were waited for; matrix products, arithmetic and copies ran while one was open for 8% of the time, Pallas kernels for 34%

commit v1 on v0

--- a/solution.py
+++ b/solution.py
@@ -445,11 +445,12 @@
 
 
 def middle_kernel(few, sc, *refs):
-    m0, m1, m2, m3, x_ref, cot_ref, vec_ref, ib_ref, weights = refs[:9]
-    outer = refs[9:13]
-    out_ref, g1_ref, d_ref, dw_ref = refs[13:17]
+    m0, m1, m2, m3, x_ref, cot_ref, vec_ref, weights = refs[:8]
+    outer = refs[8:12]
+    out_ref, g1_ref, d_ref = refs[12:15]
+    dw_ref = refs[15]
     (wo_ref, n1_ref, s1_ref, hid_ref, hidb_ref, hidt_ref, acc_ref, gp_ref, act_ref, gsb_ref, gst_ref,
-     dvec_ref) = refs[17:]
+     dvec_ref, ib_ref, move_ref) = refs[16:]
     step = pl.program_id(0)
     vec = lambda i: vec_ref[pl.ds(i, 1), :]
     mixed = (m0, m1, m2, m3)
@@ -461,10 +462,14 @@
     @pl.when(step == 0)
     def _():
         for k in range(4):
-            o = outer[k][:, 0].reshape(768, 768)
-            wo_ref[:, k * 256 : k * 256 + 256] = jnp.concatenate(
-                [o[:, h * 256 + HD : h * 256 + 2 * HD] for h in range(3)] + [jnp.zeros((768, HD), BF)], axis=1
-            )
+            wo_ref[:, k * 256 : k * 256 + 256] = outer[k][:, 0].reshape(768, 256)
+        r, l = unit_index(0), unit_index(1)
+        move_ref[...] = (r == (l % HD) // few * own_rows + (l % HD) % few).astype(F32).astype(BF)
+        unit = lax.broadcasted_iota(jnp.int32, (128, 768), 0)
+        lane = lax.broadcasted_iota(jnp.int32, (128, 768), 1)
+        for k in range(4):
+            spread = dot(wo_ref[:, k * 256 + 128 : k * 256 + 256], move_ref[...], 0, 0)
+            ib_ref[k : k + 1] = jnp.sum(jnp.where(unit - 64 == lane // HD, spread, 0.0), axis=0, keepdims=True)
         rows = x_ref[...].astype(F32) + vec(0)
         for k in range(4):
             rows = rows + dot(mixed[k][...], wo_ref[:, k * 256 : k * 256 + 192], 0, 1)
@@ -529,8 +534,6 @@
         columns = dvec_ref[...].T
         lane = lax.broadcasted_iota(jnp.int32, (768, 256), 1)
         unit = lax.broadcasted_iota(jnp.int32, (768, 256), 0)
-        r, l = unit_index(0), unit_index(1)
-        move = (r == (l % HD) // few * own_rows + (l % HD) % few).astype(F32).astype(BF)
         shared = jnp.zeros((768, 256), F32)
         for v in range(6):
             shared = jnp.where(lane == 192 + v, columns[:, v : v + 1], shared)
@@ -539,7 +542,7 @@
             d_ref[jnp.bitwise_xor(sc[6], k)] = dot(wo_ref[:, k * 256 : k * 256 + 192], lowt, 0, 0).astype(BF)
             full = jnp.concatenate([mixed[k][...], pad], axis=0)
             bias = jnp.where(lane - 200 == unit // HD, columns[:, 8 + k : 9 + k], 0.0).astype(BF)
-            tail = dot(lowt, full, 1, 1) + shared + dot(move, bias, 1, 0)
+            tail = dot(lowt, full, 1, 1) + shared + dot(move_ref[...], bias, 1, 0)
             dw_ref[:, k * 1792 + 1536 : k * 1792 + 1792] = tail.astype(BF)
 
 
@@ -547,7 +550,7 @@
     return lax.broadcasted_iota(jnp.int32, (768, 768), axis)
 
 
-def middle(sc, mixed, x, cot, vec, ib, weights, few):
+def middle(sc, mixed, x, cot, vec, weights, few):
     spec = pl.BlockSpec
     fixed = lambda shape: spec(shape, lambda i, c: (0,) * len(shape))
     once = lambda shape: spec(shape, lambda i, c: (0,) * len(shape), pipeline_mode=pl.Buffered(1))
@@ -562,9 +565,9 @@
             num_scalar_prefetch=1,
             grid=(9,),
             in_specs=[fixed((192, 512))] * 4
-            + [fixed((512, 768)), fixed((512, 768)), fixed((8, 768)), fixed((4, 768))]
+            + [fixed((512, 768)), fixed((512, 768)), fixed((8, 768))]
             + [spec((blocks, 1, rows, 1536), lambda i, c: (0, jnp.bitwise_xor(c[6], turn(i)), 0, 0))]
-            + [spec((blocks, 1, rows, 768), lambda i, c, k=k: (0, jnp.bitwise_xor(c[6], k), 0, 2)) for k in range(4)],
+            + [spec((blocks, 1, rows, 256), lambda i, c, k=k: (0, jnp.bitwise_xor(c[6], k), 0, 6)) for k in range(4)],
             out_specs=[fixed((512, 768)), fixed((512, 768)), fixed((4, 192, 512))] + [once((768, 7168))],
             scratch_shapes=[
                 pltpu.VMEM((768, 1024), BF),
@@ -579,12 +582,14 @@
                 pltpu.VMEM((512, 768), BF),
                 pltpu.VMEM((768, 512), BF),
                 pltpu.VMEM((16, 768), F32),
+                pltpu.VMEM((8, 768), F32),
+                pltpu.VMEM((768, 768), BF),
             ],
         ),
         compiler_params=params(),
         cost_estimate=LIGHT,
         name="middle",
-    )(sc, *mixed, x, cot, vec, ib, *[weights] * 5)
+    )(sc, *mixed, x, cot, vec, *[weights] * 5)
 
 
 def input_grad_kernel(heads, base_ref, w_ref, *refs):
@@ -611,7 +616,7 @@
         functools.partial(input_grad_kernel, heads),
         grid=(4,),
         out_shape=jax.ShapeDtypeStruct((512, 768), F32),
-        in_specs=[whole((512, 768)), pl.BlockSpec((blocks, 1, rows, 768), lambda k: (0, k, 0, 2))]
+        in_specs=[whole((512, 768)), pl.BlockSpec((blocks, 1, rows, 768), lambda k: (0, k, 0, 0))]
         + [pl.BlockSpec((1, 192, 512), lambda k: (k, 0, 0))] * len(packets),
         out_specs=whole((512, 768)),
         scratch_shapes=[pltpu.VMEM((768, 512), F32)],
@@ -640,13 +645,12 @@
         [by_head(query_weight), by_head(output_weight), by_head(key_weight), by_head(value_weight)], axis=2
     ).reshape(rows, heads * 256)
     small = jnp.stack([output_bias, first_gain, first_shift, outer_bias, second_gain, second_shift], axis=1)
-    inner_bias = exchange(jnp.broadcast_to(inner_bias[None], (4, few, units)))
-    biases = jnp.concatenate([query_bias, value_bias] + [pick(inner_bias, z ^ k) for k in range(4)], axis=1)
-    used = 6 + biases.shape[1]
-    biases = jnp.pad(biases, ((0, rows - few), (0, 0)))
+    biases = jnp.pad(jnp.concatenate([query_bias, value_bias], axis=1), ((0, rows - few), (0, 0)))
+    used = 6 + 2 * heads
     near = jnp.concatenate([wide, small, biases, jnp.zeros((rows, 128 - used), BF)], axis=1)
 
-    every = jnp.concatenate([inner_weight, outer_weight, wide], axis=1)
+    extra = jnp.pad(inner_bias, ((0, rows - few), (0, 64 - units)))
+    front = jnp.concatenate([inner_weight, outer_weight, output_weight, extra], axis=1)
     apart = aligned(rows)
     also = lambda a, m: jnp.concatenate([a, swap(a, "dp", m)], axis=0) if apart else a
     up, down = [tokens], [tokens]
@@ -657,11 +661,12 @@
 
     hop()
     near = also(near, 2)
-    near, up[1], down[1], every = stage(near, up[1], down[1], every)
-    every = gather_all(every)
+    near, up[1], down[1], front = stage(near, up[1], down[1], front)
+    front = gather_all(front)
     hop()
     near = also(near, 4)
-    near, up[2], down[2] = stage(near, up[2], down[2])
+    near, up[2], down[2], later = stage(near, up[2], down[2], wide)
+    full = gather_all(later)
     hop()
     if apart:
         at = [me ^ m for m in (0, 2, 4, 6, 1, 3, 5, 7)]
@@ -672,8 +677,7 @@
     vec = jnp.pad(tile[:, :6].T, ((0, 2), (0, 0)))
     tile = tile.reshape(n, rows, 128)[:, :few, 6:used].reshape(HD, used - 6).T
     blank = jnp.zeros((heads, 2 * HD), F32)
-    bias = jnp.concatenate([tile[:heads], blank, tile[heads : 2 * heads]], axis=1)[:, None, :]
-    ib = tile[2 * heads :].reshape(4, units * HD)
+    bias = jnp.concatenate([tile[:heads], blank, tile[heads:]], axis=1)[:, None, :]
     xs = [by_slot(up, down, k) for k in range(3)]
     made = [project(x, (near, where), bias) for x in xs]
     made, up[3], down[3] = stage(made, up[3], down[3])
@@ -690,15 +694,15 @@
             if s < 3:
                 mixed[s + 1] = come
             mixed[s] = swap(mixed[s], "tensor", s)
-    mixed, every = stage(mixed, every)
+    mixed, front = stage(mixed, front)
 
     sc = jnp.concatenate([counts, place])
-    out, g1, d_out, dw = middle(sc, mixed, tokens, cotangent, vec, ib, every, few)
-
-    total = lax.psum_scatter(dw, "dp", scatter_dimension=0, tiled=True)
+    out, g1, d_out, dw = middle(sc, mixed, tokens, cotangent, vec, front, few)
+
     d = exchange(d_out)
     dq0, dkv, bias0 = back_own(sc, qt[0], q[0], kv, kvt, d_out, lses[0])
-    d, dq0, dkv, bias0 = stage(d, dq0, dkv, bias0)
+    dw, full, d, dq0, dkv, bias0 = stage(dw, full, d, dq0, dkv, bias0)
+    total = lax.psum_scatter(dw, "dp", scatter_dimension=0, tiled=True)
     head = lambda h, d: back_head(h, sc, qt, q, kv, kvt, d, lses[1:], dq0, dkv, bias0, xs, few)
     packet0, *dw0 = head(0, d)
     packet0, dw0, d = stage(packet0, dw0, d)
@@ -707,39 +711,39 @@
     packet0, packet1, dw1, d = stage(packet0, packet1, dw1, d)
     packet1 = exchange(packet1)
     packet2, *dw2 = head(2, d)
-    packet1, packet2, dw2, total = stage(packet1, packet2, dw2, total)
+    packet1, packet2, dw2 = stage(packet1, packet2, dw2)
 
     packet2 = exchange(packet2)
     dws = [dw0, dw1, dw2]
     joined = lambda arrays: jnp.concatenate(arrays, axis=-1)
     if apart:
-        own_keep, own_got = joined([v[0] for v in dws]), swap(joined([v[1] for v in dws]), "dp", 1)
+        keep, got = joined([v[0] for v in dws]), swap(joined([v[1] for v in dws]), "dp", 1)
+        block = lambda m: keep[m].astype(F32) + got[m].astype(F32)
+        passed = swap(jnp.stack([block(1), block(3)]).astype(BF), "dp", 2)
+        near_by = (block(2) + passed[1].astype(F32)).astype(BF)
+        own = block(0) + passed[0].astype(F32)
     else:
-        own_keep = own_got = joined([v[0] for v in dws])
+        own, near_by = joined([v[0] for v in dws]), ()
+    ahead = input_grad(g1, full, [packet0, packet1], (0, 1))
+    ahead, own, near_by, total, packet2 = stage(ahead, own, near_by, total, packet2)
     slots = [total[:, k * 1792 : k * 1792 + 1792] for k in range(4)]
     moved = [swap(v, "tensor", k) for k, v in enumerate(slots) if k]
-    ahead = input_grad(g1, every, [packet0, packet1], (0, 1))
-    packet2, ahead, own_keep, own_got = stage(packet2, ahead, own_keep, own_got)
-    tokens_grad = input_grad(ahead, every, [packet2], (2,))
-    if apart:
-        block = lambda m: own_keep[m].astype(F32) + own_got[m].astype(F32)
-        passed = swap(jnp.stack([block(1), block(3)]).astype(BF), "dp", 2)
-        near_by = (block(2) + passed[1].astype(F32)).astype(BF)
-        own = block(0) + passed[0].astype(F32) + swap(near_by, "dp", 4).astype(F32)
-    else:
-        own = sum_rows(own_keep)
+    own = own + swap(near_by, "dp", 4).astype(F32) if apart else sum_rows(own)
+    tokens_grad = input_grad(ahead, full, [packet2], (2,))
+    side = lambda i: jnp.concatenate([own[:, h * 256 + i * HD : h * 256 + i * HD + HD] for h in range(heads)], axis=1)
+    sides = [side(i) for i in range(3)]
+    qb = jnp.stack([own[:few, h * 256 + 192] for h in range(heads)], axis=1)
+    vb = jnp.stack([own[:few, h * 256 + 193] for h in range(heads)], axis=1)
+    tokens_grad, sides, qb, vb, moved = stage(tokens_grad, sides, qb, vb, moved)
 
     sums = (slots[0].astype(F32) + moved[0].astype(F32)) + (moved[1].astype(F32) + moved[2].astype(F32))
     ffn, rest = sums[:, :1536], sums[:, 1536:]
-    side = lambda i: jnp.concatenate([own[:, h * 256 + i * HD : h * 256 + i * HD + HD] for h in range(heads)], axis=1)
     return (
         out,
         tokens_grad,
-        side(0),
-        side(1),
-        side(2),
-        jnp.stack([own[:few, h * 256 + 192] for h in range(heads)], axis=1),
-        jnp.stack([own[:few, h * 256 + 193] for h in range(heads)], axis=1),
+        *sides,
+        qb,
+        vb,
         rest[:, :192],
         rest[:, 192],
         rest[:, 193],

time: 387 us -> 362 us (0.935)
  waiting for transfers between devices: 105 us -> 87.4 us
  local copies, waits for them, and re-layouts: 24.2 us -> 18.3 us
  starting transfers between devices: 60.1 us -> 55 us
    ppermute x12, waiting for transfers between devices: 48.2 us -> 37.1 us  [swap(): return lax.ppermute(x, axis, [(i, i ^ mask) for i in range(n)])]
    all_to_all x5 -> x4, starting transfers between devices: 19.2 us -> 14.5 us  [exchange(): return lax.all_to_all(blocks, 'tensor', 0, 0)]
    all_to_all x5 -> x4, waiting for transfers between devices: 24.4 us -> 19.8 us  [exchange(): return lax.all_to_all(blocks, 'tensor', 0, 0)]
    ppermute x6, waiting for transfers between devices: 31.8 us -> 27.9 us  [shift(): lax.ppermute(x, 'tensor', [(i, i + by) for i in range(n) if 0 <= i + by <...]
    another operation x6, local copies, waits for them, and re-layouts: 4.64 us -> 0.74 us  [body(): jnp.stack([output_bias, first_gain, first_shift, outer_bias, second_gain,...]
    unnamed x48 -> x66, local copies, waits for them, and re-layouts: 9.28 us -> 8.51 us
  transfers between devices with their start and end apart: 25 -> 25, of which waited for: 16 -> 17; matrix products, arithmetic and copies ran while one was open for 8% -> 6% of each run, Pallas kernels for 34% -> 47%
where the time goes in v1:
time: 362 us; the launch traced here: 355 us
  Pallas kernels  167 us (46%)
  waiting for transfers between devices  87.4 us (24%)
  starting transfers between devices  55 us (15%)
  local copies, waits for them, and re-layouts  18.3 us (5%)
  between operations  15.2 us (4%)
  other arithmetic  11.6 us (3%)
    pallas_call x3, Pallas kernels, back_head(): pl.pallas_call(functools.partial(back_head_kernel, few, apart), out_shape...  48.3 us
    ppermute x12, waiting for transfers between devices, swap(): return lax.ppermute(x, axis, [(i, i ^ mask) for i in range(n)])  37.1 us
    pallas_call x1, Pallas kernels, middle(): pl.pallas_call(functools.partial(middle_kernel, few), out_shape=[shape((5...  36.1 us
    pallas_call x4, Pallas kernels, attend(): pl.pallas_call(attend_kernel, out_shape=[jax.ShapeDtypeStruct((heads * HD...  34.2 us
    ppermute x6, waiting for transfers between devices, shift(): lax.ppermute(x, 'tensor', [(i, i + by) for i in range(n) if 0 <= i + by <...  27.9 us
    ppermute x12, starting transfers between devices, swap(): return lax.ppermute(x, axis, [(i, i ^ mask) for i in range(n)])  23.4 us
    all_to_all x4, waiting for transfers between devices, exchange(): return lax.all_to_all(blocks, 'tensor', 0, 0)  19.8 us
    pallas_call x4, Pallas kernels, project(): pl.pallas_call(project_kernel, out_shape=[jax.ShapeDtypeStruct(s, BF) for...  19.7 us
  transfers between devices with their start and end apart: 25, of which 17 were waited for; matrix products, arithmetic and copies ran while one was open for 6% of the time, Pallas kernels for 47%

profile of v1, /device:TPU:0, one launch (start us, length us, event | category | flops | bytes accessed | tf_op | source)
XLA Modules:
  0.0 354.7 jit_solution(13598476759480500155)
XLA Ops:
  7.4 5.1 %collective-permute-start.1 = (bf16[512,768]{1,0:T(8,128)(2,1)}, bf16[512,768]{1,0:T(8,128)(2,1)S(1)}, u32[]{:S(2)}, u32[]{:S(2)}) collective-permute-start(bf16[512,768]{1,0:T(8,128)(2,1)} %refs_23_.5), channel_id=1, source_target_pairs={{0,1},{1,2},{2,3},{4,5},{5,6},{6,7},{8,9},{9,10},{10,11},{12,13},{... | collective-permute-start | bytes 2359304 | tf_op jit(solution)/shard_map/ppermute | solution.py:56
  24.8 4.7 %collective-permute-done.1 = bf16[512,768]{1,0:T(8,128)(2,1)S(1)} collective-permute-done((bf16[512,768]{1,0:T(8,128)(2,1)}, bf16[512,768]{1,0:T(8,128)(2,1)S(1)}, u32[]{:S(2)}, u32[]{:S(2)}) %collective-permute-start.1) | collective-permute-done | bytes 786464 | tf_op jit(solution)/shard_map/ppermute | solution.py:56
  40.0 9.3 %collective-permute-done.3 = bf16[192,896]{1,0:T(8,128)(2,1)S(1)} collective-permute-done((bf16[192,896]{1,0:T(8,128)(2,1)S(1)}, bf16[192,896]{1,0:T(8,128)(2,1)S(1)}, u32[]{:S(2)}, u32[]{:S(2)}) %collective-permute-start.3) | collective-permute-done | bytes 344096 | tf_op jit(solution)/shard_map/ppermute | solution.py:35
  49.4 10.7 %collective-permute-done.4 = bf16[512,768]{1,0:T(8,128)(2,1)S(1)} collective-permute-done((bf16[512,768]{1,0:T(8,128)(2,1)S(1)}, bf16[512,768]{1,0:T(8,128)(2,1)S(1)}, u32[]{:S(2)}, u32[]{:S(2)}) %collective-permute-start.4) | collective-permute-done | bytes 786464 | tf_op jit(solution)/shard_map/ppermute | solution.py:56
  80.6 4.9 %project.4 = (bf16[3,128,512]{2,1,0:T(8,128)(2,1)}, bf16[3,512,128]{2,1,0:T(8,128)(2,1)}, bf16[3,512,128]{2,1,0:T(8,128)(2,1)}, bf16[3,128,512]{2,1,0:T(8,128)(2,1)}) custom-call(s32[8]{0:T(128)} %broadcast_multiply_fusion.where, bf16[512,768]{1,0:T(8,128)(2,1)} %refs_23_.5, f32[3,1,256]{2,1,0:T(1,128)} %broadcast_in_dim.11.b_ref, ...), custom_call_target="tpu_custom_call" | custom-call | flops 1 | bytes 1 | tf_op jit(solution)/shard_map/project/pallas_call | solution.py:234
  85.5 4.9 %project.6 = (bf16[3,128,512]{2,1,0:T(8,128)(2,1)}, bf16[3,512,128]{2,1,0:T(8,128)(2,1)}, bf16[3,512,128]{2,1,0:T(8,128)(2,1)}, bf16[3,128,512]{2,1,0:T(8,128)(2,1)}) custom-call(s32[8]{0:T(128)} %broadcast_multiply_fusion.where, bf16[512,768]{1,0:T(8,128)(2,1)} %broadcast_select_fusion.x_ref.refs_25_, f32[3,1,256]{2,1,0:T(1,128)} %broadcast_in_dim.11.b_ref, ...), custom_call_target="tpu_custom_call" | custom-call | flops 1 | bytes 1 | tf_op jit(solution)/shard_map/project/pallas_call | solution.py:234
  90.4 4.9 %project.5 = (bf16[3,128,512]{2,1,0:T(8,128)(2,1)}, bf16[3,512,128]{2,1,0:T(8,128)(2,1)}, bf16[3,512,128]{2,1,0:T(8,128)(2,1)}, bf16[3,128,512]{2,1,0:T(8,128)(2,1)}) custom-call(s32[8]{0:T(128)} %broadcast_multiply_fusion.where, bf16[512,768]{1,0:T(8,128)(2,1)} %broadcast_select_fusion.1.x_ref.refs_24_, f32[3,1,256]{2,1,0:T(1,128)} %broadcast_in_dim.11.b_ref, ...), custom_call_target="tpu_custom_call" | custom-call | flops 1 | bytes 1 | tf_op jit(solution)/shard_map/project/pallas_call | solution.py:234
  103.1 4.9 %project.7 = (bf16[3,128,512]{2,1,0:T(8,128)(2,1)}, bf16[3,512,128]{2,1,0:T(8,128)(2,1)}, bf16[3,512,128]{2,1,0:T(8,128)(2,1)}, bf16[3,128,512]{2,1,0:T(8,128)(2,1)}) custom-call(s32[8]{0:T(128)} %broadcast_multiply_fusion.where, bf16[512,768]{1,0:T(8,128)(2,1)} %select_select_fusion.x_ref.refs_26_, f32[3,1,256]{2,1,0:T(1,128)} %broadcast_in_dim.11.b_ref, ...), custom_call_target="tpu_custom_call" | custom-call | flops 1 | bytes 1 | tf_op jit(solution)/shard_map/project/pallas_call | solution.py:234
  108.0 8.5 %attend.4 = (bf16[192,512]{1,0:T(8,128)(2,1)}, f32[3,1,512]{2,1,0:T(1,128)}) custom-call(s32[4]{0:T(128)} %subtract_clamp_fusion.counts, bf16[3,128,512]{2,1,0:T(8,128)(2,1)} %get-tuple-element.145.qt_ref.refs_2_, bf16[3,512,128]{2,1,0:T(8,128)(2,1)} %get-tuple-element.146.k0.refs_0_.refs_6_, bf16[3,512,128]{2,1,0:T(8,128)(2,1)} %get-tuple-element.147.k1.refs_1_.refs_7_, ...), custom_call_target="tpu_custom_call" | custom-call | flops 1 | bytes 1 | tf_op jit(solution)/shard_map/attend/pallas_call | solution.py:273
  118.8 8.5 %attend.5 = (bf16[192,512]{1,0:T(8,128)(2,1)}, f32[3,1,512]{2,1,0:T(1,128)}) custom-call(s32[4]{0:T(128)} %subtract_clamp_fusion.counts, bf16[3,128,512]{2,1,0:T(8,128)(2,1)} %get-tuple-element.156.qt_ref.refs_1_, bf16[3,512,128]{2,1,0:T(8,128)(2,1)} %get-tuple-element.146.k0.refs_0_.refs_6_, bf16[3,512,128]{2,1,0:T(8,128)(2,1)} %get-tuple-element.147.k1.refs_1_.refs_7_, ...), custom_call_target="tpu_custom_call" | custom-call | flops 1 | bytes 1 | tf_op jit(solution)/shard_map/attend/pallas_call | solution.py:273
  129.3 10.5 %collective-permute-start.10 = (bf16[192,512]{1,0:T(8,128)(2,1)}, bf16[192,512]{1,0:T(8,128)(2,1)S(1)}, u32[]{:S(2)}, u32[]{:S(2)}) collective-permute-start(bf16[192,512]{1,0:T(8,128)(2,1)} %get-tuple-element.163), channel_id=1, source_target_pairs={{0,2},{1,3},{2,0},{3,1},{4,6},{5,7},{6,4},{7,5},{8,10},{9,11},{10,... | collective-permute-start | bytes 589832 | tf_op jit(solution)/shard_map/ppermute | solution.py:35
  140.4 8.7 %attend.6 = (bf16[192,512]{1,0:T(8,128)(2,1)}, f32[3,1,512]{2,1,0:T(1,128)}) custom-call(s32[4]{0:T(128)} %subtract_clamp_fusion.counts, bf16[3,128,512]{2,1,0:T(8,128)(2,1)} %get-tuple-element.160.qt_ref.refs_0_, bf16[3,512,128]{2,1,0:T(8,128)(2,1)} %get-tuple-element.146.k0.refs_0_.refs_6_, bf16[3,512,128]{2,1,0:T(8,128)(2,1)} %get-tuple-element.147.k1.refs_1_.refs_7_, ...), custom_call_target="tpu_custom_call" | custom-call | flops 1 | bytes 1 | tf_op jit(solution)/shard_map/attend/pallas_call | solution.py:273
  149.9 8.5 %attend.7 = (bf16[192,512]{1,0:T(8,128)(2,1)}, f32[3,1,512]{2,1,0:T(1,128)}) custom-call(s32[4]{0:T(128)} %subtract_clamp_fusion.counts, bf16[3,128,512]{2,1,0:T(8,128)(2,1)} %get-tuple-element.164.qt_ref, bf16[3,512,128]{2,1,0:T(8,128)(2,1)} %get-tuple-element.146.k0.refs_0_.refs_6_, bf16[3,512,128]{2,1,0:T(8,128)(2,1)} %get-tuple-element.147.k1.refs_1_.refs_7_, ...), custom_call_target="tpu_custom_call" | custom-call | flops 1 | bytes 1 | tf_op jit(solution)/shard_map/attend/pallas_call | solution.py:273
  159.1 36.1 %middle.1 = (bf16[512,768]{1,0:T(8,128)(2,1)}, f32[512,768]{1,0:T(8,128)}, bf16[4,192,512]{2,1,0:T(8,128)(2,1)}, bf16[768,7168]{1,0:T(8,128)(2,1)}) custom-call(s32[7]{0:T(128)} %pad_add_fusion.sc.counts, bf16[192,512]{1,0:T(8,128)(2,1)} %get-tuple-element.170.refs_0_, bf16[192,512]{1,0:T(8,128)(2,1)} %copy-done.15, bf16[192,512]{1,0:T(8,128)(2,1)} %copy-done.14, ...), custom_call_target="tpu_custom_call" | custom-call | flops 1 | bytes 1 | tf_op jit(solution)/shard_map/middle/pallas_call | solution.py:560
  198.8 13.6 %back_own.1 = (bf16[3,64,512]{2,1,0:T(8,128)(2,1)}, f32[3,4,512,128]{3,2,1,0:T(8,128)}, f32[3,64,1]{2,1,0:T(8,128)}) custom-call(s32[7]{0:T(128)} %pad_add_fusion.sc.counts, bf16[3,128,512]{2,1,0:T(8,128)(2,1)} %get-tuple-element.164.qt_ref, bf16[3,512,128]{2,1,0:T(8,128)(2,1)} %get-tuple-element.180.q_ref, ...), custom_call_target="tpu_custom_call" | custom-call | flops 1 | bytes 1 | tf_op jit(solution)/shard_map/back_own/pallas_call | solution.py:326
  214.9 8.1 %all-to-all-done.refs_14_.refs_15_.refs_16_ = bf16[4,192,512]{2,1,0:T(8,128)(2,1)S(1)} async-done(((bf16[4,192,512]{2,1,0:T(8,128)(2,1)}), bf16[4,192,512]{2,1,0:T(8,128)(2,1)S(1)}, u32[]{:S(2)}, u32[]{:S(2)}) %all-to-all-start) | async-done | bytes 786464 | tf_op jit(solution)/shard_map/all_to_all | solution.py:72
  223.9 16.5 %back_head.3 = (bf16[4,192,512]{2,1,0:T(8,128)(2,1)}, bf16[4,96,256]{2,1,0:T(8,128)(2,1)}, bf16[4,96,256]{2,1,0:T(8,128)(2,1)}) custom-call(s32[7]{0:T(128)} %pad_add_fusion.sc.counts, bf16[3,128,512]{2,1,0:T(8,128)(2,1)} %get-tuple-element.160.qt_ref.refs_0_, bf16[3,128,512]{2,1,0:T(8,128)(2,1)} %get-tuple-element.156.qt_ref.refs_1_, ...), custom_call_target="tpu_custom_call" | custom-call | flops 1 | bytes 1 | tf_op jit(solution)/shard_map/back_head/pallas_call | solution.py:400
  244.1 15.8 %back_head.4 = (bf16[4,192,512]{2,1,0:T(8,128)(2,1)}, bf16[4,96,256]{2,1,0:T(8,128)(2,1)}, bf16[4,96,256]{2,1,0:T(8,128)(2,1)}) custom-call(s32[7]{0:T(128)} %pad_add_fusion.sc.counts, bf16[3,128,512]{2,1,0:T(8,128)(2,1)} %get-tuple-element.160.qt_ref.refs_0_, bf16[3,128,512]{2,1,0:T(8,128)(2,1)} %get-tuple-element.156.qt_ref.refs_1_, ...), custom_call_target="tpu_custom_call" | custom-call | flops 1 | bytes 1 | tf_op jit(solution)/shard_map/back_head/pallas_call | solution.py:400
  267.0 16.0 %back_head.5 = (bf16[4,192,512]{2,1,0:T(8,128)(2,1)}, bf16[4,96,256]{2,1,0:T(8,128)(2,1)}, bf16[4,96,256]{2,1,0:T(8,128)(2,1)}) custom-call(s32[7]{0:T(128)} %pad_add_fusion.sc.counts, bf16[3,128,512]{2,1,0:T(8,128)(2,1)} %get-tuple-element.160.qt_ref.refs_0_, bf16[3,128,512]{2,1,0:T(8,128)(2,1)} %get-tuple-element.156.qt_ref.refs_1_, ...), custom_call_target="tpu_custom_call" | custom-call | flops 1 | bytes 1 | tf_op jit(solution)/shard_map/back_head/pallas_call | solution.py:400
  293.4 7.0 %input_grad.2.base_ref = f32[512,768]{1,0:T(8,128)} custom-call(f32[512,768]{1,0:T(8,128)} %get-tuple-element.176.base_ref, bf16[8,4,96,768]{3,2,1,0:T(8,128)(2,1)} %bitcast.41, bf16[4,192,512]{2,1,0:T(8,128)(2,1)} %copy-done.3, bf16[4,192,512]{2,1,0:T(8,128)(2,1)} %copy-done.4), custom_call_target="tpu_custom_call" | custom-call | flops 1 | bytes 1 | tf_op jit(solution)/shard_map/input_grad/pallas_call | solution.py:615
  300.4 7.6 %collective-permute-done.13 = bf16[2,96,768]{2,1,0:T(8,128)(2,1)S(1)} collective-permute-done((bf16[2,96,768]{2,1,0:T(8,128)(2,1)S(1)}, bf16[2,96,768]{2,1,0:T(8,128)(2,1)S(1)}, u32[]{:S(2)}, u32[]{:S(2)}) %collective-permute-start.13) | collective-permute-done | bytes 294944 | tf_op jit(solution)/shard_map/ppermute | solution.py:35
  308.1 4.6 %all-to-all-done.3.refs_0_ = bf16[4,192,512]{2,1,0:T(8,128)(2,1)S(1)} async-done(((bf16[4,192,512]{2,1,0:T(8,128)(2,1)}), bf16[4,192,512]{2,1,0:T(8,128)(2,1)S(1)}, u32[]{:S(2)}, u32[]{:S(2)}) %all-to-all-start.3) | async-done | bytes 786464 | tf_op jit(solution)/shard_map/all_to_all | solution.py:72
  319.8 6.1 %input_grad.3 = f32[512,768]{1,0:T(8,128)} custom-call(f32[512,768]{1,0:T(8,128)} %input_grad.2.base_ref, bf16[8,4,96,768]{3,2,1,0:T(8,128)(2,1)} %bitcast.42, bf16[4,192,512]{2,1,0:T(8,128)(2,1)} %copy-done.5), custom_call_target="tpu_custom_call" | custom-call | flops 1 | bytes 1 | tf_op jit(solution)/shard_map/input_grad/pallas_call | solution.py:615
  331.2 11.3 %collective-permute-done.16 = bf16[96,1792]{1,0:T(8,128)(2,1)S(1)} collective-permute-done((bf16[96,1792]{1,0:T(8,128)(2,1)S(1)}, bf16[96,1792]{1,0:T(8,128)(2,1)S(1)}, u32[]{:S(2)}, u32[]{:S(2)}) %collective-permute-start.16) | collective-permute-done | bytes 344096 | tf_op jit(solution)/shard_map/ppermute | solution.py:35
  (164 shorter events, 102.6 us)
Async XLA Ops:
  7.3 151.1 %all-gather.5.cloned.1.call-start = ((), (), s32[]{:S(2)}) async-start(), calls=%async_computation.6 | async-start | bytes 11354112 | tf_op jit(solution)/shard_map/all_gather | solution.py:82
  7.4 22.2 %collective-permute-start.1 = (bf16[512,768]{1,0:T(8,128)(2,1)}, bf16[512,768]{1,0:T(8,128)(2,1)S(1)}, u32[]{:S(2)}, u32[]{:S(2)}) collective-permute-start(bf16[512,768]{1,0:T(8,128)(2,1)} %refs_23_.5), channel_id=1, source_target_pairs={{0,1},{1,2},{2,3},{4,5},{5,6},{6,7},{8,9},{9,10},{10,11},{12,13},{... | collective-permute-start | bytes 2359304 | tf_op jit(solution)/shard_map/ppermute | solution.py:56
  12.5 21.1 %collective-permute-start.2 = (bf16[512,768]{1,0:T(8,128)(2,1)}, bf16[512,768]{1,0:T(8,128)(2,1)S(1)}, u32[]{:S(2)}, u32[]{:S(2)}) collective-permute-start(bf16[512,768]{1,0:T(8,128)(2,1)} %refs_23_.5), channel_id=1, source_target_pairs={{1,0},{2,1},{3,2},{5,4},{6,5},{7,6},{9,8},{10,9},{11,10},{13,12},{... | collective-permute-start | bytes 2359304 | tf_op jit(solution)/shard_map/ppermute | solution.py:56
  18.9 5.9 %collective-permute-start = (bf16[96,896]{1,0:T(8,128)(2,1)S(1)}, bf16[96,896]{1,0:T(8,128)(2,1)S(1)}, u32[]{:S(2)}, u32[]{:S(2)}) collective-permute-start(bf16[96,896]{1,0:T(8,128)(2,1)S(1)} %concatenate.38), channel_id=1, source_target_pairs={{0,8},{4,12},{8,0},{12,4},{16,24},{20,28},{24,16},{28,20},{1,9},{5... | collective-permute-start | bytes 516104 | tf_op jit(solution)/shard_map/ppermute | solution.py:35
  33.6 181.3 %all-gather.7.cloned.1.call-start = ((), (), s32[]{:S(2)}) async-start(), calls=%async_computation.7 | async-start | bytes 4866048 | tf_op jit(solution)/shard_map/all_gather | solution.py:82
  33.7 26.4 %collective-permute-start.4 = (bf16[512,768]{1,0:T(8,128)(2,1)S(1)}, bf16[512,768]{1,0:T(8,128)(2,1)S(1)}, u32[]{:S(2)}, u32[]{:S(2)}) collective-permute-start(bf16[512,768]{1,0:T(8,128)(2,1)S(1)} %collective-permute-done.1), channel_id=1, source_target_pairs={{0,1},{1,2},{2,3},{4,5},{5,6},{6,7},{8,9},{9,10},{10,11},{12,13},{... | collective-permute-start | bytes 2359304 | tf_op jit(solution)/shard_map/ppermute | solution.py:56
  37.2 27.2 %collective-permute-start.5 = (bf16[512,768]{1,0:T(8,128)(2,1)S(1)}, bf16[512,768]{1,0:T(8,128)(2,1)}, u32[]{:S(2)}, u32[]{:S(2)}) collective-permute-start(bf16[512,768]{1,0:T(8,128)(2,1)S(1)} %collective-permute-done.2), channel_id=1, source_target_pairs={{1,0},{2,1},{3,2},{5,4},{6,5},{7,6},{9,8},{10,9},{11,10},{13,12},{... | collective-permute-start | bytes 2359304 | tf_op jit(solution)/shard_map/ppermute | solution.py:56
  38.5 10.9 %collective-permute-start.3 = (bf16[192,896]{1,0:T(8,128)(2,1)S(1)}, bf16[192,896]{1,0:T(8,128)(2,1)S(1)}, u32[]{:S(2)}, u32[]{:S(2)}) collective-permute-start(bf16[192,896]{1,0:T(8,128)(2,1)S(1)} %pad_maximum_fusion.2), channel_id=1, source_target_pairs={{0,16},{4,20},{8,24},{12,28},{16,0},{20,4},{24,8},{28,12},{1,17},{... | collective-permute-start | bytes 1032200 | tf_op jit(solution)/shard_map/ppermute | solution.py:35
  65.3 9.4 %collective-permute-start.6 = (bf16[384,896]{1,0:T(8,128)(2,1)S(1)}, bf16[384,896]{1,0:T(8,128)(2,1)S(1)}, u32[]{:S(2)}, u32[]{:S(2)}) collective-permute-start(bf16[384,896]{1,0:T(8,128)(2,1)S(1)} %pad_maximum_fusion.refs_0_), channel_id=1, source_target_pairs={{0,4},{4,0},{8,12},{12,8},{16,20},{20,16},{24,28},{28,24},{1,5},{5... | collective-permute-start | bytes 2064392 | tf_op jit(solution)/shard_map/ppermute | solution.py:35
  66.8 31.0 %collective-permute-start.7 = (bf16[512,768]{1,0:T(8,128)(2,1)}, bf16[512,768]{1,0:T(8,128)(2,1)}, u32[]{:S(2)}, u32[]{:S(2)}) collective-permute-start(bf16[512,768]{1,0:T(8,128)(2,1)} %copy-done.6), channel_id=1, source_target_pairs={{0,1},{1,2},{2,3},{4,5},{5,6},{6,7},{8,9},{9,10},{10,11},{12,13},{... | collective-permute-start | bytes 2359304 | tf_op jit(solution)/shard_map/ppermute | solution.py:56
  71.2 29.2 %collective-permute-start.8 = (bf16[512,768]{1,0:T(8,128)(2,1)}, bf16[512,768]{1,0:T(8,128)(2,1)}, u32[]{:S(2)}, u32[]{:S(2)}) collective-permute-start(bf16[512,768]{1,0:T(8,128)(2,1)} %collective-permute-done.5), channel_id=1, source_target_pairs={{1,0},{2,1},{3,2},{5,4},{6,5},{7,6},{9,8},{10,9},{11,10},{13,12},{... | collective-permute-start | bytes 2359304 | tf_op jit(solution)/shard_map/ppermute | solution.py:56
  116.5 12.7 %collective-permute-start.9 = (bf16[192,512]{1,0:T(8,128)(2,1)}, bf16[192,512]{1,0:T(8,128)(2,1)S(1)}, u32[]{:S(2)}, u32[]{:S(2)}) collective-permute-start(bf16[192,512]{1,0:T(8,128)(2,1)} %get-tuple-element.159), channel_id=1, source_target_pairs={{0,3},{1,2},{2,1},{3,0},{4,7},{5,6},{6,5},{7,4},{8,11},{9,10},{10,... | collective-permute-start | bytes 589832 | tf_op jit(solution)/shard_map/ppermute | solution.py:35
  129.3 19.9 %collective-permute-start.10 = (bf16[192,512]{1,0:T(8,128)(2,1)}, bf16[192,512]{1,0:T(8,128)(2,1)S(1)}, u32[]{:S(2)}, u32[]{:S(2)}) collective-permute-start(bf16[192,512]{1,0:T(8,128)(2,1)} %get-tuple-element.163), channel_id=1, source_target_pairs={{0,2},{1,3},{2,0},{3,1},{4,6},{5,7},{6,4},{7,5},{8,10},{9,11},{10,... | collective-permute-start | bytes 589832 | tf_op jit(solution)/shard_map/ppermute | solution.py:35
  149.2 9.2 %collective-permute-start.11 = (bf16[192,512]{1,0:T(8,128)(2,1)}, bf16[192,512]{1,0:T(8,128)(2,1)S(1)}, u32[]{:S(2)}, u32[]{:S(2)}) collective-permute-start(bf16[192,512]{1,0:T(8,128)(2,1)} %get-tuple-element.166), channel_id=1, source_target_pairs={{0,1},{1,0},{2,3},{3,2},{4,5},{5,4},{6,7},{7,6},{8,9},{9,8},{10,11... | collective-permute-start | bytes 589832 | tf_op jit(solution)/shard_map/ppermute | solution.py:35
  195.2 27.9 %all-to-all-start = ((bf16[4,192,512]{2,1,0:T(8,128)(2,1)}), bf16[4,192,512]{2,1,0:T(8,128)(2,1)S(1)}, u32[]{:S(2)}, u32[]{:S(2)}) async-start(bf16[4,192,512]{2,1,0:T(8,128)(2,1)} %get-tuple-element.179.refs_8_), calls=%async_computation | async-start | bytes 1572864 | tf_op jit(solution)/shard_map/all_to_all | solution.py:72
  198.8 113.9 %reduce-scatter.2.cloned.1.call-start = ((), (), s32[]{:S(2)}) async-start(), calls=%async_computation.5 | async-start | bytes 12386304 | tf_op jit(solution)/shard_map/reduce_scatter | solution.py:705
  240.5 23.0 %all-to-all-start.1 = ((bf16[4,192,512]{2,1,0:T(8,128)(2,1)}), bf16[4,192,512]{2,1,0:T(8,128)(2,1)S(1)}, u32[]{:S(2)}, u32[]{:S(2)}) async-start(bf16[4,192,512]{2,1,0:T(8,128)(2,1)} %get-tuple-element.199), calls=%async_computation.1 | async-start | bytes 1572864 | tf_op jit(solution)/shard_map/all_to_all | solution.py:72
  263.5 23.1 %all-to-all-start.2 = ((bf16[4,192,512]{2,1,0:T(8,128)(2,1)}), bf16[4,192,512]{2,1,0:T(8,128)(2,1)S(1)}, u32[]{:S(2)}, u32[]{:S(2)}) async-start(bf16[4,192,512]{2,1,0:T(8,128)(2,1)} %get-tuple-element.205), calls=%async_computation.2 | async-start | bytes 1572864 | tf_op jit(solution)/shard_map/all_to_all | solution.py:72
  288.0 24.7 %all-to-all-start.3 = ((bf16[4,192,512]{2,1,0:T(8,128)(2,1)}), bf16[4,192,512]{2,1,0:T(8,128)(2,1)S(1)}, u32[]{:S(2)}, u32[]{:S(2)}) async-start(bf16[4,192,512]{2,1,0:T(8,128)(2,1)} %get-tuple-element.218), calls=%async_computation.4 | async-start | bytes 1572864 | tf_op jit(solution)/shard_map/all_to_all | solution.py:72
  292.0 16.1 %collective-permute-start.13 = (bf16[2,96,768]{2,1,0:T(8,128)(2,1)S(1)}, bf16[2,96,768]{2,1,0:T(8,128)(2,1)S(1)}, u32[]{:S(2)}, u32[]{:S(2)}) collective-permute-start(bf16[2,96,768]{2,1,0:T(8,128)(2,1)S(1)} %pad_maximum_fusion.3), channel_id=1, source_target_pairs={{0,8},{4,12},{8,0},{12,4},{16,24},{20,28},{24,16},{28,20},{1,9},{5... | collective-permute-start | bytes 884744 | tf_op jit(solution)/shard_map/ppermute | solution.py:35
  312.7 13.2 %collective-permute-start.14 = (bf16[96,768]{1,0:T(8,128)(2,1)S(1)}, bf16[96,768]{1,0:T(8,128)(2,1)S(1)}, u32[]{:S(2)}, u32[]{:S(2)}) collective-permute-start(bf16[96,768]{1,0:T(8,128)(2,1)S(1)} %get-tuple-element.222), channel_id=1, source_target_pairs={{0,16},{4,20},{8,24},{12,28},{16,0},{20,4},{24,8},{28,12},{1,17},{... | collective-permute-start | bytes 442376 | tf_op jit(solution)/shard_map/ppermute | solution.py:35
  315.4 15.9 %collective-permute-start.15 = (bf16[96,1792]{1,0:T(8,128)(2,1)S(1)}, bf16[96,1792]{1,0:T(8,128)(2,1)S(1)}, u32[]{:S(2)}, u32[]{:S(2)}) collective-permute-start(bf16[96,1792]{1,0:T(8,128)(2,1)S(1)} %get-tuple-element.294), channel_id=1, source_target_pairs={{0,1},{1,0},{2,3},{3,2},{4,5},{5,4},{6,7},{7,6},{8,9},{9,8},{10,11... | collective-permute-start | bytes 1032200 | tf_op jit(solution)/shard_map/ppermute | solution.py:35
  315.9 26.6 %collective-permute-start.16 = (bf16[96,1792]{1,0:T(8,128)(2,1)S(1)}, bf16[96,1792]{1,0:T(8,128)(2,1)S(1)}, u32[]{:S(2)}, u32[]{:S(2)}) collective-permute-start(bf16[96,1792]{1,0:T(8,128)(2,1)S(1)} %get-tuple-element.293), channel_id=1, source_target_pairs={{0,2},{1,3},{2,0},{3,1},{4,6},{5,7},{6,4},{7,5},{8,10},{9,11},{10,... | collective-permute-start | bytes 1032200 | tf_op jit(solution)/shard_map/ppermute | solution.py:35
  318.3 24.2 %collective-permute-start.17 = (bf16[96,1792]{1,0:T(8,128)(2,1)S(1)}, bf16[96,1792]{1,0:T(8,128)(2,1)S(1)}, u32[]{:S(2)}, u32[]{:S(2)}) collective-permute-start(bf16[96,1792]{1,0:T(8,128)(2,1)S(1)} %get-tuple-element.292), channel_id=1, source_target_pairs={{0,3},{1,2},{2,1},{3,0},{4,7},{5,6},{6,5},{7,4},{8,11},{9,10},{10,... | collective-permute-start | bytes 1032200 | tf_op jit(solution)/shard_map/ppermute | solution.py:35
  (29 other events, 298.0 us)
Sparse Core Ops, SparseCore 0:
  33.7 109.2 all-gather.4
  145.8 69.0 all-gather.6
  223.2 88.3 reduce-scatter.1

commit v2 on v1

--- a/solution.py
+++ b/solution.py
@@ -424,7 +424,7 @@
             ],
         ),
         compiler_params=params(),
-        cost_estimate=LIGHT,
+        cost_estimate=pl.CostEstimate(flops=10**11, transcendentals=0, bytes_accessed=1),
         name="back_head",
     )(sc, *qt[1:], *q[1:], *kv, *kvt, *[dts] * 3, *lses, dq0, dkv, bias0, *xs)
 
@@ -450,7 +450,7 @@
     out_ref, g1_ref, d_ref = refs[12:15]
     dw_ref = refs[15]
     (wo_ref, n1_ref, s1_ref, hid_ref, hidb_ref, hidt_ref, acc_ref, gp_ref, act_ref, gsb_ref, gst_ref,
-     dvec_ref, ib_ref, move_ref) = refs[16:]
+     dvec_ref, ib_ref, move_ref, part_ref, tail_ref, part_sem, tail_sem) = refs[16:]
     step = pl.program_id(0)
     vec = lambda i: vec_ref[pl.ds(i, 1), :]
     mixed = (m0, m1, m2, m3)
@@ -514,9 +514,18 @@
         dvec_ref[pl.ds(8 + k, 1), :] = jnp.sum(gi, axis=0, keepdims=True)
         low = gi.astype(BF)
         acc_ref[...] += dot(low, inner(), 1, 1)
-        at = pl.multiple_of(k * 1792, 256)
-        dw_ref[:, pl.ds(at, 768)] = dot(hidt_ref[...], low, 1, 0).astype(BF)
-        dw_ref[:, pl.ds(at + 768, 768)] = dot(gst_ref[...], act_ref[k], 1, 0).astype(BF)
+        turn = lax.rem(step, 2)
+        leave = lambda k, turn: pltpu.make_async_copy(
+            part_ref.at[turn], dw_ref.at[:, pl.ds(pl.multiple_of(k * 1792, 256), 1536)], part_sem.at[turn]
+        )
+
+        @pl.when(step >= 6)
+        def _():
+            leave(k + 2, turn).wait()
+
+        part_ref[turn, :, :768] = dot(hidt_ref[...], low, 1, 0).astype(BF)
+        part_ref[turn, :, 768:] = dot(gst_ref[...], act_ref[k], 1, 0).astype(BF)
+        leave(k, turn).start()
 
     @pl.when(step == 8)
     def _():
@@ -543,7 +552,19 @@
             full = jnp.concatenate([mixed[k][...], pad], axis=0)
             bias = jnp.where(lane - 200 == unit // HD, columns[:, 8 + k : 9 + k], 0.0).astype(BF)
             tail = dot(lowt, full, 1, 1) + shared + dot(move_ref[...], bias, 1, 0)
-            dw_ref[:, k * 1792 + 1536 : k * 1792 + 1792] = tail.astype(BF)
+            tail_ref[k] = tail.astype(BF)
+            pltpu.make_async_copy(
+                tail_ref.at[k], dw_ref.at[:, k * 1792 + 1536 : k * 1792 + 1792], tail_sem.at[k]
+            ).start()
+        for k in range(4):
+            pltpu.make_async_copy(
+                tail_ref.at[k], dw_ref.at[:, k * 1792 + 1536 : k * 1792 + 1792], tail_sem.at[k]
+            ).wait()
+        for k in (1, 0):
+            turn = (7 - k) % 2
+            pltpu.make_async_copy(
+                part_ref.at[turn], dw_ref.at[:, k * 1792 : k * 1792 + 1536], part_sem.at[turn]
+            ).wait()
 
 
 def unit_index(axis):
@@ -568,7 +589,7 @@
             + [fixed((512, 768)), fixed((512, 768)), fixed((8, 768))]
             + [spec((blocks, 1, rows, 1536), lambda i, c: (0, jnp.bitwise_xor(c[6], turn(i)), 0, 0))]
             + [spec((blocks, 1, rows, 256), lambda i, c, k=k: (0, jnp.bitwise_xor(c[6], k), 0, 6)) for k in range(4)],
-            out_specs=[fixed((512, 768)), fixed((512, 768)), fixed((4, 192, 512))] + [once((768, 7168))],
+            out_specs=[fixed((512, 768)), fixed((512, 768)), fixed((4, 192, 512))] + [spec(memory_space=pl.ANY)],
             scratch_shapes=[
                 pltpu.VMEM((768, 1024), BF),
                 pltpu.VMEM((512, 768), F32),
@@ -584,6 +605,10 @@
                 pltpu.VMEM((16, 768), F32),
                 pltpu.VMEM((8, 768), F32),
                 pltpu.VMEM((768, 768), BF),
+                pltpu.VMEM((2, 768, 1536), BF),
+                pltpu.VMEM((4, 768, 256), BF),
+                pltpu.SemaphoreType.DMA((2,)),
+                pltpu.SemaphoreType.DMA((4,)),
             ],
         ),
         compiler_params=params(),
@@ -701,8 +726,9 @@
 
     d = exchange(d_out)
     dq0, dkv, bias0 = back_own(sc, qt[0], q[0], kv, kvt, d_out, lses[0])
-    dw, full, d, dq0, dkv, bias0 = stage(dw, full, d, dq0, dkv, bias0)
+    dw, full, bias0 = stage(dw, full, bias0)
     total = lax.psum_scatter(dw, "dp", scatter_dimension=0, tiled=True)
+    d, dq0, dkv, bias0 = stage(d, dq0, dkv, bias0)
     head = lambda h, d: back_head(h, sc, qt, q, kv, kvt, d, lses[1:], dq0, dkv, bias0, xs, few)
     packet0, *dw0 = head(0, d)
     packet0, dw0, d = stage(packet0, dw0, d)
@@ -725,7 +751,7 @@
     else:
         own, near_by = joined([v[0] for v in dws]), ()
     ahead = input_grad(g1, full, [packet0, packet1], (0, 1))
-    ahead, own, near_by, total, packet2 = stage(ahead, own, near_by, total, packet2)
+    ahead, own, near_by, total = stage(ahead, own, near_by, total)
     slots = [total[:, k * 1792 : k * 1792 + 1792] for k in range(4)]
     moved = [swap(v, "tensor", k) for k, v in enumerate(slots) if k]
     own = own + swap(near_by, "dp", 4).astype(F32) if apart else sum_rows(own)

time: 362 us -> 357 us (0.986)
  the two profiles are of different devices: /device:TPU:0 before, /device:TPU:8 now
where the time goes in v2:
time: 357 us; the launch traced here: 353 us
  Pallas kernels  165 us (46%)
  waiting for transfers between devices  82.4 us (23%)
  starting transfers between devices  58 us (16%)
  local copies, waits for them, and re-layouts  20.2 us (6%)
  between operations  15.2 us (4%)
  other arithmetic  11.8 us (3%)
    pallas_call x3, Pallas kernels, back_head(): pl.pallas_call(functools.partial(back_head_kernel, few, apart), out_shape...  48.3 us
    ppermute x12, waiting for transfers between devices, swap(): return lax.ppermute(x, axis, [(i, i ^ mask) for i in range(n)])  47.8 us
    pallas_call x1, Pallas kernels, middle(): pl.pallas_call(functools.partial(middle_kernel, few), out_shape=[shape((5...  34.1 us
    pallas_call x4, Pallas kernels, attend(): pl.pallas_call(attend_kernel, out_shape=[jax.ShapeDtypeStruct((heads * HD...  34 us
    all_to_all x4, starting transfers between devices, exchange(): return lax.all_to_all(blocks, 'tensor', 0, 0)  25.3 us
    ppermute x6, waiting for transfers between devices, shift(): lax.ppermute(x, 'tensor', [(i, i + by) for i in range(n) if 0 <= i + by <...  24.7 us
    pallas_call x4, Pallas kernels, project(): pl.pallas_call(project_kernel, out_shape=[jax.ShapeDtypeStruct(s, BF) for...  19.6 us
    ppermute x6, starting transfers between devices, shift(): lax.ppermute(x, 'tensor', [(i, i + by) for i in range(n) if 0 <= i + by <...  18.8 us
  transfers between devices with their start and end apart: 25, of which 18 were waited for; matrix products, arithmetic and copies ran while one was open for 6% of the time, Pallas kernels for 47%

profile of v2, /device:TPU:8, one launch (start us, length us, event | category | flops | bytes accessed | tf_op | source)
XLA Modules:
  0.0 352.6 jit_solution(9931070940955920559)
XLA Ops:
  39.7 9.0 %collective-permute-done.3 = bf16[192,896]{1,0:T(8,128)(2,1)S(1)} collective-permute-done((bf16[192,896]{1,0:T(8,128)(2,1)S(1)}, bf16[192,896]{1,0:T(8,128)(2,1)S(1)}, u32[]{:S(2)}, u32[]{:S(2)}) %collective-permute-start.3) | collective-permute-done | bytes 344096 | tf_op jit(solution)/shard_map/ppermute | solution.py:35
  48.7 10.8 %collective-permute-done.4 = bf16[512,768]{1,0:T(8,128)(2,1)S(1)} collective-permute-done((bf16[512,768]{1,0:T(8,128)(2,1)S(1)}, bf16[512,768]{1,0:T(8,128)(2,1)S(1)}, u32[]{:S(2)}, u32[]{:S(2)}) %collective-permute-start.4) | collective-permute-done | bytes 786464 | tf_op jit(solution)/shard_map/ppermute | solution.py:56
  80.3 4.9 %project.4 = (bf16[3,128,512]{2,1,0:T(8,128)(2,1)}, bf16[3,512,128]{2,1,0:T(8,128)(2,1)}, bf16[3,512,128]{2,1,0:T(8,128)(2,1)}, bf16[3,128,512]{2,1,0:T(8,128)(2,1)}) custom-call(s32[8]{0:T(128)} %broadcast_multiply_fusion.where, bf16[512,768]{1,0:T(8,128)(2,1)} %refs_23_.5, f32[3,1,256]{2,1,0:T(1,128)} %broadcast_in_dim.11.b_ref, bf16[384,896]{1,0:T(8,128)(2,1)} %copy-done, ...), custom_call_target="tpu_custom_call" | custom-call | flops 1 | bytes 1 | tf_op jit(solution)/shard_map/project/pallas_call | solution.py:234
  85.2 4.9 %project.6 = (bf16[3,128,512]{2,1,0:T(8,128)(2,1)}, bf16[3,512,128]{2,1,0:T(8,128)(2,1)}, bf16[3,512,128]{2,1,0:T(8,128)(2,1)}, bf16[3,128,512]{2,1,0:T(8,128)(2,1)}) custom-call(s32[8]{0:T(128)} %broadcast_multiply_fusion.where, bf16[512,768]{1,0:T(8,128)(2,1)} %broadcast_select_fusion.x_ref.refs_25_, f32[3,1,256]{2,1,0:T(1,128)} %broadcast_in_dim.11.b_ref, ...), custom_call_target="tpu_custom_call" | custom-call | flops 1 | bytes 1 | tf_op jit(solution)/shard_map/project/pallas_call | solution.py:234
  90.1 4.9 %project.5 = (bf16[3,128,512]{2,1,0:T(8,128)(2,1)}, bf16[3,512,128]{2,1,0:T(8,128)(2,1)}, bf16[3,512,128]{2,1,0:T(8,128)(2,1)}, bf16[3,128,512]{2,1,0:T(8,128)(2,1)}) custom-call(s32[8]{0:T(128)} %broadcast_multiply_fusion.where, bf16[512,768]{1,0:T(8,128)(2,1)} %broadcast_select_fusion.1.x_ref.refs_24_, f32[3,1,256]{2,1,0:T(1,128)} %broadcast_in_dim.11.b_ref, ...), custom_call_target="tpu_custom_call" | custom-call | flops 1 | bytes 1 | tf_op jit(solution)/shard_map/project/pallas_call | solution.py:234
  101.4 4.9 %project.7 = (bf16[3,128,512]{2,1,0:T(8,128)(2,1)}, bf16[3,512,128]{2,1,0:T(8,128)(2,1)}, bf16[3,512,128]{2,1,0:T(8,128)(2,1)}, bf16[3,128,512]{2,1,0:T(8,128)(2,1)}) custom-call(s32[8]{0:T(128)} %broadcast_multiply_fusion.where, bf16[512,768]{1,0:T(8,128)(2,1)} %select_select_fusion.x_ref.refs_26_, f32[3,1,256]{2,1,0:T(1,128)} %broadcast_in_dim.11.b_ref, ...), custom_call_target="tpu_custom_call" | custom-call | flops 1 | bytes 1 | tf_op jit(solution)/shard_map/project/pallas_call | solution.py:234
  106.3 8.5 %attend.4 = (bf16[192,512]{1,0:T(8,128)(2,1)}, f32[3,1,512]{2,1,0:T(1,128)}) custom-call(s32[4]{0:T(128)} %subtract_clamp_fusion.counts, bf16[3,128,512]{2,1,0:T(8,128)(2,1)} %get-tuple-element.145.qt_ref.refs_2_, bf16[3,512,128]{2,1,0:T(8,128)(2,1)} %get-tuple-element.146.k0.refs_0_.refs_6_, bf16[3,512,128]{2,1,0:T(8,128)(2,1)} %get-tuple-element.147.k1.refs_1_.refs_7_, ...), custom_call_target="tpu_custom_call" | custom-call | flops 1 | bytes 1 | tf_op jit(solution)/shard_map/attend/pallas_call | solution.py:273
  116.4 8.5 %attend.5 = (bf16[192,512]{1,0:T(8,128)(2,1)}, f32[3,1,512]{2,1,0:T(1,128)}) custom-call(s32[4]{0:T(128)} %subtract_clamp_fusion.counts, bf16[3,128,512]{2,1,0:T(8,128)(2,1)} %get-tuple-element.156.qt_ref.refs_1_, bf16[3,512,128]{2,1,0:T(8,128)(2,1)} %get-tuple-element.146.k0.refs_0_.refs_6_, bf16[3,512,128]{2,1,0:T(8,128)(2,1)} %get-tuple-element.147.k1.refs_1_.refs_7_, ...), custom_call_target="tpu_custom_call" | custom-call | flops 1 | bytes 1 | tf_op jit(solution)/shard_map/attend/pallas_call | solution.py:273
  124.9 11.6 %collective-permute-done.9.refs_3_ = bf16[192,512]{1,0:T(8,128)(2,1)S(1)} collective-permute-done((bf16[192,512]{1,0:T(8,128)(2,1)}, bf16[192,512]{1,0:T(8,128)(2,1)S(1)}, u32[]{:S(2)}, u32[]{:S(2)}) %collective-permute-start.9) | collective-permute-done | bytes 196640 | tf_op jit(solution)/shard_map/ppermute | solution.py:35
  137.1 8.5 %attend.6 = (bf16[192,512]{1,0:T(8,128)(2,1)}, f32[3,1,512]{2,1,0:T(1,128)}) custom-call(s32[4]{0:T(128)} %subtract_clamp_fusion.counts, bf16[3,128,512]{2,1,0:T(8,128)(2,1)} %get-tuple-element.160.qt_ref.refs_0_, bf16[3,512,128]{2,1,0:T(8,128)(2,1)} %get-tuple-element.146.k0.refs_0_.refs_6_, bf16[3,512,128]{2,1,0:T(8,128)(2,1)} %get-tuple-element.147.k1.refs_1_.refs_7_, ...), custom_call_target="tpu_custom_call" | custom-call | flops 1 | bytes 1 | tf_op jit(solution)/shard_map/attend/pallas_call | solution.py:273
  148.8 8.5 %attend.7 = (bf16[192,512]{1,0:T(8,128)(2,1)}, f32[3,1,512]{2,1,0:T(1,128)}) custom-call(s32[4]{0:T(128)} %subtract_clamp_fusion.counts, bf16[3,128,512]{2,1,0:T(8,128)(2,1)} %get-tuple-element.164.qt_ref, bf16[3,512,128]{2,1,0:T(8,128)(2,1)} %get-tuple-element.146.k0.refs_0_.refs_6_, bf16[3,512,128]{2,1,0:T(8,128)(2,1)} %get-tuple-element.147.k1.refs_1_.refs_7_, ...), custom_call_target="tpu_custom_call" | custom-call | flops 1 | bytes 1 | tf_op jit(solution)/shard_map/attend/pallas_call | solution.py:273
  158.0 34.1 %middle.1 = (bf16[512,768]{1,0:T(8,128)(2,1)}, f32[512,768]{1,0:T(8,128)}, bf16[4,192,512]{2,1,0:T(8,128)(2,1)}, bf16[768,7168]{1,0:T(8,128)(2,1)}) custom-call(s32[7]{0:T(128)} %pad_add_fusion.sc.counts, bf16[192,512]{1,0:T(8,128)(2,1)} %get-tuple-element.170.refs_0_, bf16[192,512]{1,0:T(8,128)(2,1)} %copy-done.14, bf16[192,512]{1,0:T(8,128)(2,1)} %copy-done.13, ...), custom_call_target="tpu_custom_call" | custom-call | flops 1 | bytes 1 | tf_op jit(solution)/shard_map/middle/pallas_call | solution.py:581
  195.9 13.6 %back_own.1 = (bf16[3,64,512]{2,1,0:T(8,128)(2,1)}, f32[3,4,512,128]{3,2,1,0:T(8,128)}, f32[3,64,1]{2,1,0:T(8,128)}) custom-call(s32[7]{0:T(128)} %pad_add_fusion.sc.counts, bf16[3,128,512]{2,1,0:T(8,128)(2,1)} %get-tuple-element.164.qt_ref, bf16[3,512,128]{2,1,0:T(8,128)(2,1)} %get-tuple-element.179.q_ref, ...), custom_call_target="tpu_custom_call" | custom-call | flops 1 | bytes 1 | tf_op jit(solution)/shard_map/back_own/pallas_call | solution.py:326
  210.5 7.0 %all-to-all-done.refs_14_.refs_15_.refs_16_ = bf16[4,192,512]{2,1,0:T(8,128)(2,1)S(1)} async-done(((bf16[4,192,512]{2,1,0:T(8,128)(2,1)}), bf16[4,192,512]{2,1,0:T(8,128)(2,1)S(1)}, u32[]{:S(2)}, u32[]{:S(2)}) %all-to-all-start) | async-done | bytes 786464 | tf_op jit(solution)/shard_map/all_to_all | solution.py:72
  218.4 16.7 %back_head.3 = (bf16[4,192,512]{2,1,0:T(8,128)(2,1)}, bf16[4,96,256]{2,1,0:T(8,128)(2,1)}, bf16[4,96,256]{2,1,0:T(8,128)(2,1)}) custom-call(s32[7]{0:T(128)} %pad_add_fusion.sc.counts, bf16[3,128,512]{2,1,0:T(8,128)(2,1)} %get-tuple-element.160.qt_ref.refs_0_, bf16[3,128,512]{2,1,0:T(8,128)(2,1)} %get-tuple-element.156.qt_ref.refs_1_, ...), custom_call_target="tpu_custom_call" | custom-call | flops 99999997952 | bytes 1 | tf_op jit(solution)/shard_map/back_head/pallas_call | solution.py:400
  235.2 7.9 %all-to-all-start.1 = ((bf16[4,192,512]{2,1,0:T(8,128)(2,1)}), bf16[4,192,512]{2,1,0:T(8,128)(2,1)S(1)}, u32[]{:S(2)}, u32[]{:S(2)}) async-start(bf16[4,192,512]{2,1,0:T(8,128)(2,1)} %get-tuple-element.200), calls=%async_computation.1 | async-start | bytes 1572864 | tf_op jit(solution)/shard_map/all_to_all | solution.py:72
  243.1 15.8 %back_head.4 = (bf16[4,192,512]{2,1,0:T(8,128)(2,1)}, bf16[4,96,256]{2,1,0:T(8,128)(2,1)}, bf16[4,96,256]{2,1,0:T(8,128)(2,1)}) custom-call(s32[7]{0:T(128)} %pad_add_fusion.sc.counts, bf16[3,128,512]{2,1,0:T(8,128)(2,1)} %get-tuple-element.160.qt_ref.refs_0_, bf16[3,128,512]{2,1,0:T(8,128)(2,1)} %get-tuple-element.156.qt_ref.refs_1_, ...), custom_call_target="tpu_custom_call" | custom-call | flops 99999997952 | bytes 1 | tf_op jit(solution)/shard_map/back_head/pallas_call | solution.py:400
  259.8 6.7 %all-to-all-start.2 = ((bf16[4,192,512]{2,1,0:T(8,128)(2,1)}), bf16[4,192,512]{2,1,0:T(8,128)(2,1)S(1)}, u32[]{:S(2)}, u32[]{:S(2)}) async-start(bf16[4,192,512]{2,1,0:T(8,128)(2,1)} %get-tuple-element.206), calls=%async_computation.2 | async-start | bytes 1572864 | tf_op jit(solution)/shard_map/all_to_all | solution.py:72
  266.6 15.8 %back_head.5 = (bf16[4,192,512]{2,1,0:T(8,128)(2,1)}, bf16[4,96,256]{2,1,0:T(8,128)(2,1)}, bf16[4,96,256]{2,1,0:T(8,128)(2,1)}) custom-call(s32[7]{0:T(128)} %pad_add_fusion.sc.counts, bf16[3,128,512]{2,1,0:T(8,128)(2,1)} %get-tuple-element.160.qt_ref.refs_0_, bf16[3,128,512]{2,1,0:T(8,128)(2,1)} %get-tuple-element.156.qt_ref.refs_1_, ...), custom_call_target="tpu_custom_call" | custom-call | flops 99999997952 | bytes 1 | tf_op jit(solution)/shard_map/back_head/pallas_call | solution.py:400
  284.3 7.0 %all-to-all-start.3 = ((bf16[4,192,512]{2,1,0:T(8,128)(2,1)}), bf16[4,192,512]{2,1,0:T(8,128)(2,1)S(1)}, u32[]{:S(2)}, u32[]{:S(2)}) async-start(bf16[4,192,512]{2,1,0:T(8,128)(2,1)} %get-tuple-element.220), calls=%async_computation.4 | async-start | bytes 1572864 | tf_op jit(solution)/shard_map/all_to_all | solution.py:72
  293.8 7.0 %input_grad.2.base_ref = f32[512,768]{1,0:T(8,128)} custom-call(f32[512,768]{1,0:T(8,128)} %get-tuple-element.176.base_ref, bf16[8,4,96,768]{3,2,1,0:T(8,128)(2,1)} %bitcast.41, bf16[4,192,512]{2,1,0:T(8,128)(2,1)} %copy-done.2, bf16[4,192,512]{2,1,0:T(8,128)(2,1)} %copy-done.3), custom_call_target="tpu_custom_call" | custom-call | flops 1 | bytes 1 | tf_op jit(solution)/shard_map/input_grad/pallas_call | solution.py:640
  310.4 6.1 %input_grad.3 = f32[512,768]{1,0:T(8,128)} custom-call(f32[512,768]{1,0:T(8,128)} %input_grad.2.base_ref, bf16[8,4,96,768]{3,2,1,0:T(8,128)(2,1)} %bitcast.42, bf16[4,192,512]{2,1,0:T(8,128)(2,1)} %copy-done.4), custom_call_target="tpu_custom_call" | custom-call | flops 1 | bytes 1 | tf_op jit(solution)/shard_map/input_grad/pallas_call | solution.py:640
  322.5 9.4 %collective-permute-done.16 = bf16[96,1792]{1,0:T(8,128)(2,1)S(1)} collective-permute-done((bf16[96,1792]{1,0:T(8,128)(2,1)S(1)}, bf16[96,1792]{1,0:T(8,128)(2,1)S(1)}, u32[]{:S(2)}, u32[]{:S(2)}) %collective-permute-start.16) | collective-permute-done | bytes 344096 | tf_op jit(solution)/shard_map/ppermute | solution.py:35
  331.9 8.5 %collective-permute-done.17 = bf16[96,1792]{1,0:T(8,128)(2,1)S(1)} collective-permute-done((bf16[96,1792]{1,0:T(8,128)(2,1)S(1)}, bf16[96,1792]{1,0:T(8,128)(2,1)S(1)}, u32[]{:S(2)}, u32[]{:S(2)}) %collective-permute-start.17) | collective-permute-done | bytes 344096 | tf_op jit(solution)/shard_map/ppermute | solution.py:35
  (162 shorter events, 96.7 us)
Async XLA Ops:
  7.3 150.0 %all-gather.5.cloned.1.call-start = ((), (), s32[]{:S(2)}) async-start(), calls=%async_computation.6 | async-start | bytes 11354112 | tf_op jit(solution)/shard_map/all_gather | solution.py:82
  7.4 21.5 %collective-permute-start.1 = (bf16[512,768]{1,0:T(8,128)(2,1)}, bf16[512,768]{1,0:T(8,128)(2,1)S(1)}, u32[]{:S(2)}, u32[]{:S(2)}) collective-permute-start(bf16[512,768]{1,0:T(8,128)(2,1)} %refs_23_.5), channel_id=1, source_target_pairs={{0,1},{1,2},{2,3},{4,5},{5,6},{6,7},{8,9},{9,10},{10,11},{12,13},{... | collective-permute-start | bytes 2359304 | tf_op jit(solution)/shard_map/ppermute | solution.py:56
  11.0 21.1 %collective-permute-start.2 = (bf16[512,768]{1,0:T(8,128)(2,1)}, bf16[512,768]{1,0:T(8,128)(2,1)S(1)}, u32[]{:S(2)}, u32[]{:S(2)}) collective-permute-start(bf16[512,768]{1,0:T(8,128)(2,1)} %refs_23_.5), channel_id=1, source_target_pairs={{1,0},{2,1},{3,2},{5,4},{6,5},{7,6},{9,8},{10,9},{11,10},{13,12},{... | collective-permute-start | bytes 2359304 | tf_op jit(solution)/shard_map/ppermute | solution.py:56
  32.1 178.4 %all-gather.7.cloned.1.call-start = ((), (), s32[]{:S(2)}) async-start(), calls=%async_computation.7 | async-start | bytes 4866048 | tf_op jit(solution)/shard_map/all_gather | solution.py:82
  32.2 27.4 %collective-permute-start.4 = (bf16[512,768]{1,0:T(8,128)(2,1)S(1)}, bf16[512,768]{1,0:T(8,128)(2,1)S(1)}, u32[]{:S(2)}, u32[]{:S(2)}) collective-permute-start(bf16[512,768]{1,0:T(8,128)(2,1)S(1)} %collective-permute-done.1), channel_id=1, source_target_pairs={{0,1},{1,2},{2,3},{4,5},{5,6},{6,7},{8,9},{9,10},{10,11},{12,13},{... | collective-permute-start | bytes 2359304 | tf_op jit(solution)/shard_map/ppermute | solution.py:56
  35.7 27.2 %collective-permute-start.5 = (bf16[512,768]{1,0:T(8,128)(2,1)S(1)}, bf16[512,768]{1,0:T(8,128)(2,1)}, u32[]{:S(2)}, u32[]{:S(2)}) collective-permute-start(bf16[512,768]{1,0:T(8,128)(2,1)S(1)} %collective-permute-done.2), channel_id=1, source_target_pairs={{1,0},{2,1},{3,2},{5,4},{6,5},{7,6},{9,8},{10,9},{11,10},{13,12},{... | collective-permute-start | bytes 2359304 | tf_op jit(solution)/shard_map/ppermute | solution.py:56
  38.1 10.6 %collective-permute-start.3 = (bf16[192,896]{1,0:T(8,128)(2,1)S(1)}, bf16[192,896]{1,0:T(8,128)(2,1)S(1)}, u32[]{:S(2)}, u32[]{:S(2)}) collective-permute-start(bf16[192,896]{1,0:T(8,128)(2,1)S(1)} %pad_maximum_fusion.2), channel_id=1, source_target_pairs={{0,16},{4,20},{8,24},{12,28},{16,0},{20,4},{24,8},{28,12},{1,17},{... | collective-permute-start | bytes 1032200 | tf_op jit(solution)/shard_map/ppermute | solution.py:35
  63.9 10.5 %collective-permute-start.6 = (bf16[384,896]{1,0:T(8,128)(2,1)S(1)}, bf16[384,896]{1,0:T(8,128)(2,1)S(1)}, u32[]{:S(2)}, u32[]{:S(2)}) collective-permute-start(bf16[384,896]{1,0:T(8,128)(2,1)S(1)} %pad_maximum_fusion.refs_0_), channel_id=1, source_target_pairs={{0,4},{4,0},{8,12},{12,8},{16,20},{20,16},{24,28},{28,24},{1,5},{5... | collective-permute-start | bytes 2064392 | tf_op jit(solution)/shard_map/ppermute | solution.py:35
  65.4 31.9 %collective-permute-start.7 = (bf16[512,768]{1,0:T(8,128)(2,1)}, bf16[512,768]{1,0:T(8,128)(2,1)}, u32[]{:S(2)}, u32[]{:S(2)}) collective-permute-start(bf16[512,768]{1,0:T(8,128)(2,1)} %copy-done.5), channel_id=1, source_target_pairs={{0,1},{1,2},{2,3},{4,5},{5,6},{6,7},{8,9},{9,10},{10,11},{12,13},{... | collective-permute-start | bytes 2359304 | tf_op jit(solution)/shard_map/ppermute | solution.py:56
  67.6 30.9 %collective-permute-start.8 = (bf16[512,768]{1,0:T(8,128)(2,1)}, bf16[512,768]{1,0:T(8,128)(2,1)}, u32[]{:S(2)}, u32[]{:S(2)}) collective-permute-start(bf16[512,768]{1,0:T(8,128)(2,1)} %collective-permute-done.5), channel_id=1, source_target_pairs={{1,0},{2,1},{3,2},{5,4},{6,5},{7,6},{9,8},{10,9},{11,10},{13,12},{... | collective-permute-start | bytes 2359304 | tf_op jit(solution)/shard_map/ppermute | solution.py:56
  114.8 21.6 %collective-permute-start.9 = (bf16[192,512]{1,0:T(8,128)(2,1)}, bf16[192,512]{1,0:T(8,128)(2,1)S(1)}, u32[]{:S(2)}, u32[]{:S(2)}) collective-permute-start(bf16[192,512]{1,0:T(8,128)(2,1)} %get-tuple-element.159), channel_id=1, source_target_pairs={{0,3},{1,2},{2,1},{3,0},{4,7},{5,6},{6,5},{7,4},{8,11},{9,10},{10,... | collective-permute-start | bytes 589832 | tf_op jit(solution)/shard_map/ppermute | solution.py:35
  136.5 9.2 %collective-permute-start.10 = (bf16[192,512]{1,0:T(8,128)(2,1)}, bf16[192,512]{1,0:T(8,128)(2,1)S(1)}, u32[]{:S(2)}, u32[]{:S(2)}) collective-permute-start(bf16[192,512]{1,0:T(8,128)(2,1)} %get-tuple-element.163), channel_id=1, source_target_pairs={{0,2},{1,3},{2,0},{3,1},{4,6},{5,7},{6,4},{7,5},{8,10},{9,11},{10,... | collective-permute-start | bytes 589832 | tf_op jit(solution)/shard_map/ppermute | solution.py:35
  145.7 11.6 %collective-permute-start.11 = (bf16[192,512]{1,0:T(8,128)(2,1)}, bf16[192,512]{1,0:T(8,128)(2,1)S(1)}, u32[]{:S(2)}, u32[]{:S(2)}) collective-permute-start(bf16[192,512]{1,0:T(8,128)(2,1)} %get-tuple-element.166), channel_id=1, source_target_pairs={{0,1},{1,0},{2,3},{3,2},{4,5},{5,4},{6,7},{7,6},{8,9},{9,8},{10,11... | collective-permute-start | bytes 589832 | tf_op jit(solution)/shard_map/ppermute | solution.py:35
  192.1 25.5 %all-to-all-start = ((bf16[4,192,512]{2,1,0:T(8,128)(2,1)}), bf16[4,192,512]{2,1,0:T(8,128)(2,1)S(1)}, u32[]{:S(2)}, u32[]{:S(2)}) async-start(bf16[4,192,512]{2,1,0:T(8,128)(2,1)} %get-tuple-element.180.refs_8_), calls=%async_computation | async-start | bytes 1572864 | tf_op jit(solution)/shard_map/all_to_all | solution.py:72
  195.9 107.0 %reduce-scatter.2.cloned.1.call-start = ((), (), s32[]{:S(2)}) async-start(), calls=%async_computation.5 | async-start | bytes 12386304 | tf_op jit(solution)/shard_map/reduce_scatter | solution.py:730
  235.2 24.6 %all-to-all-start.1 = ((bf16[4,192,512]{2,1,0:T(8,128)(2,1)}), bf16[4,192,512]{2,1,0:T(8,128)(2,1)S(1)}, u32[]{:S(2)}, u32[]{:S(2)}) async-start(bf16[4,192,512]{2,1,0:T(8,128)(2,1)} %get-tuple-element.200), calls=%async_computation.1 | async-start | bytes 1572864 | tf_op jit(solution)/shard_map/all_to_all | solution.py:72
  259.8 23.1 %all-to-all-start.2 = ((bf16[4,192,512]{2,1,0:T(8,128)(2,1)}), bf16[4,192,512]{2,1,0:T(8,128)(2,1)S(1)}, u32[]{:S(2)}, u32[]{:S(2)}) async-start(bf16[4,192,512]{2,1,0:T(8,128)(2,1)} %get-tuple-element.206), calls=%async_computation.2 | async-start | bytes 1572864 | tf_op jit(solution)/shard_map/all_to_all | solution.py:72
  284.2 8.1 %collective-permute-start.12 = (bf16[4,96,768]{2,1,0:T(8,128)(2,1)S(1)}, bf16[4,96,768]{2,1,0:T(8,128)(2,1)S(1)}, u32[]{:S(2)}, u32[]{:S(2)}) collective-permute-start(bf16[4,96,768]{2,1,0:T(8,128)(2,1)S(1)} %pad_maximum_fusion.1), channel_id=1, source_target_pairs={{0,4},{4,0},{8,12},{12,8},{16,20},{20,16},{24,28},{28,24},{1,5},{5... | collective-permute-start | bytes 1769480 | tf_op jit(solution)/shard_map/ppermute | solution.py:35
  284.3 25.2 %all-to-all-start.3 = ((bf16[4,192,512]{2,1,0:T(8,128)(2,1)}), bf16[4,192,512]{2,1,0:T(8,128)(2,1)S(1)}, u32[]{:S(2)}, u32[]{:S(2)}) async-start(bf16[4,192,512]{2,1,0:T(8,128)(2,1)} %get-tuple-element.220), calls=%async_computation.4 | async-start | bytes 1572864 | tf_op jit(solution)/shard_map/all_to_all | solution.py:72
  292.4 10.3 %collective-permute-start.13 = (bf16[2,96,768]{2,1,0:T(8,128)(2,1)S(1)}, bf16[2,96,768]{2,1,0:T(8,128)(2,1)S(1)}, u32[]{:S(2)}, u32[]{:S(2)}) collective-permute-start(bf16[2,96,768]{2,1,0:T(8,128)(2,1)S(1)} %pad_maximum_fusion.3), channel_id=1, source_target_pairs={{0,8},{4,12},{8,0},{12,4},{16,24},{20,28},{24,16},{28,20},{1,9},{5... | collective-permute-start | bytes 884744 | tf_op jit(solution)/shard_map/ppermute | solution.py:35
  302.8 13.6 %collective-permute-start.14 = (bf16[96,768]{1,0:T(8,128)(2,1)S(1)}, bf16[96,768]{1,0:T(8,128)(2,1)S(1)}, u32[]{:S(2)}, u32[]{:S(2)}) collective-permute-start(bf16[96,768]{1,0:T(8,128)(2,1)S(1)} %get-tuple-element.222), channel_id=1, source_target_pairs={{0,16},{4,20},{8,24},{12,28},{16,0},{20,4},{24,8},{28,12},{1,17},{... | collective-permute-start | bytes 442376 | tf_op jit(solution)/shard_map/ppermute | solution.py:35
  305.6 16.9 %collective-permute-start.15 = (bf16[96,1792]{1,0:T(8,128)(2,1)S(1)}, bf16[96,1792]{1,0:T(8,128)(2,1)S(1)}, u32[]{:S(2)}, u32[]{:S(2)}) collective-permute-start(bf16[96,1792]{1,0:T(8,128)(2,1)S(1)} %get-tuple-element.294), channel_id=1, source_target_pairs={{0,1},{1,0},{2,3},{3,2},{4,5},{5,4},{6,7},{7,6},{8,9},{9,8},{10,11... | collective-permute-start | bytes 1032200 | tf_op jit(solution)/shard_map/ppermute | solution.py:35
  306.2 25.7 %collective-permute-start.16 = (bf16[96,1792]{1,0:T(8,128)(2,1)S(1)}, bf16[96,1792]{1,0:T(8,128)(2,1)S(1)}, u32[]{:S(2)}, u32[]{:S(2)}) collective-permute-start(bf16[96,1792]{1,0:T(8,128)(2,1)S(1)} %get-tuple-element.293), channel_id=1, source_target_pairs={{0,2},{1,3},{2,0},{3,1},{4,6},{5,7},{6,4},{7,5},{8,10},{9,11},{10,... | collective-permute-start | bytes 1032200 | tf_op jit(solution)/shard_map/ppermute | solution.py:35
  308.6 31.8 %collective-permute-start.17 = (bf16[96,1792]{1,0:T(8,128)(2,1)S(1)}, bf16[96,1792]{1,0:T(8,128)(2,1)S(1)}, u32[]{:S(2)}, u32[]{:S(2)}) collective-permute-start(bf16[96,1792]{1,0:T(8,128)(2,1)S(1)} %get-tuple-element.292), channel_id=1, source_target_pairs={{0,3},{1,2},{2,1},{3,0},{4,7},{5,6},{6,5},{7,4},{8,11},{9,10},{10,... | collective-permute-start | bytes 1032200 | tf_op jit(solution)/shard_map/ppermute | solution.py:35
  (28 other events, 279.6 us)
Sparse Core Ops, SparseCore 0:
  32.2 103.9 all-gather.4
  139.0 71.4 all-gather.6
  214.1 84.9 reduce-scatter.1
